TPU v7x, 256 devices: a whole 4x4x8 slice. The times are simulated.
256 devices in a mesh: band: 4 (over x_lo, core), grid: 64 (over z, y, x_hi).
Axes of the slice: x: 4 (x_hi: 2, x_lo: 2; x = x_hi * 2 + x_lo), y: 4, z: 8, core: 2. Of those that a mesh axis runs over, the one named last changes fastest.
Arguments:
- orbitals: float32 [256, 256, 8, 128], P('band', 'grid'), may hold values from -6 to 6
- potential: float32 [256, 8, 128], P('grid'), may hold values from 0 to 1.5
Outputs:
- orthonormal: float32 [256, 256, 8, 128], P('band', 'grid')
All inputs are finite; a program needn't handle non-finite values.
Results may differ from a plain program's by a relative error of at most 0.000071.
Values sent between devices are 32-bit elements; how exact they have to be, the bound alone decides.
A program may use at most 64 MiB of HBM per device.

v0:
```python
import jax
import jax.numpy as jnp
from jax import lax
from jax.sharding import PartitionSpec as P

COEFS = (-205.0 / 72.0, 8.0 / 5.0, -1.0 / 5.0, 8.0 / 315.0, -1.0 / 560.0)
CENTER = 8.0
HALF = 4.0


def with_halo(block, sides, width):
    for axis, dim in sides:
        count = lax.axis_size(axis)
        forward = [(i, i + 1) for i in range(count - 1)]
        forward.append((count - 1, 0))
        backward = [(target, source) for source, target in forward]
        low = lax.ppermute(
            lax.slice_in_dim(block, block.shape[dim] - width, None, axis=dim), axis, forward
        )
        high = lax.ppermute(lax.slice_in_dim(block, 0, width, axis=dim), axis, backward)
        block = jnp.concatenate([low, block, high], axis=dim)
    return block


def periodic_pad(field, axis):
    count = field.shape[axis]
    head = lax.slice_in_dim(field, count - 4, count, axis=axis)
    tail = lax.slice_in_dim(field, 0, 4, axis=axis)
    return jnp.concatenate([head, field, tail], axis=axis)


def add_axis(lap, padded, axis, count):
    for shift in range(1, 5):
        upper = lax.slice_in_dim(padded, 4 + shift, 4 + shift + count, axis=axis)
        lower = lax.slice_in_dim(padded, 4 - shift, 4 - shift + count, axis=axis)
        lap = lap + COEFS[shift] * (upper + lower)
    return lap


def ham_slab(field, potential):
    padded_x = with_halo(field, (("grid", 1),), 4)
    lap = 3.0 * COEFS[0] * field
    lap = add_axis(lap, padded_x, 1, field.shape[1])
    lap = add_axis(lap, periodic_pad(field, 2), 2, field.shape[2])
    lap = add_axis(lap, periodic_pad(field, 3), 3, field.shape[3])
    return -0.5 * lap + potential[None] * field


def chebyshev(field, potential, operator):
    prev = field
    cur = (operator(field, potential) - CENTER * field) / HALF
    nxt = 2.0 * (operator(cur, potential) - CENTER * cur) / HALF - prev
    prev, cur = (cur, nxt)
    return cur


def lower_inverse(margin):
    factor = jnp.linalg.cholesky(margin)
    ident = jnp.eye(margin.shape[0], dtype=jnp.float32)
    return lax.linalg.triangular_solve(factor, ident, left_side=True, lower=True)


def body(orbitals, potential):
    cur = chebyshev(orbitals, potential, ham_slab)
    orb_count, planes, rows_y, rows_z = cur.shape
    groups = lax.axis_size("band")
    ncells = planes * lax.axis_size("grid") * rows_y * rows_z
    gathered = lax.all_gather(cur, "band", axis=0, tiled=True)
    own = cur.reshape(orb_count, -1)
    whole = gathered.reshape(orb_count * groups, -1)
    partial_value = jnp.dot(
        own, whole.T, precision=lax.Precision.HIGHEST, preferred_element_type=jnp.float32
    )
    rows = lax.psum(partial_value, "grid") / float(ncells)
    margin = lax.all_gather(rows, "band", axis=0, tiled=True)
    inverse = lower_inverse(margin)
    mine = lax.dynamic_slice_in_dim(inverse, lax.axis_index("band") * orb_count, orb_count, 0)
    result = jnp.dot(
        mine, whole, precision=lax.Precision.HIGHEST, preferred_element_type=jnp.float32
    )
    return result.reshape(orb_count, planes, rows_y, rows_z)


def solution(mesh):
    return jax.shard_map(
        body,
        mesh=mesh,
        in_specs=(P("band", "grid", None, None), P("grid", None, None)),
        out_specs=P("band", "grid", None, None),
        check_vma=False,
    )
```

profile of v0, /device:TPU:1, one launch (start us, length us, event | category | flops | bytes accessed | tf_op | source)
XLA Modules:
  0.0 881.5 jit_solution(5420446859480414676)
XLA Ops:
  6.5 1.8 copy.42
  8.4 3.7 collective-permute-start.1
  12.0 7.8 collective-permute-start
  20.3 36.0 %collective-permute-done.1 = f32[64,4,8,128]{3,0,2,1:T(8,128)S(1)} collective-permute-done((f32[64,4,8,128]{3,0,2,1:T(8,128)S(1)}, f32[64,4,8,128]{3,0,2,1:T(8,128)S(1)}, u32[]{:S(2)}, u32[]{:S(2)}) %collective-permute-start.1) | collective-permute-done | bytes 1048608 | tf_op jit(solution)/shard_map/ppermute | solution.py:17
  57.1 1.2 collective-permute-done
  58.4 4.5 broadcast_multiply_fusion
  62.9 7.7 collective-permute-start.2
  71.1 21.6 %collective-permute-done.2 = f32[64,4,8,128]{3,0,2,1:T(8,128)S(1)} collective-permute-done((f32[64,4,8,128]{3,0,2,1:T(8,128)S(1)}, f32[64,4,8,128]{3,0,2,1:T(8,128)S(1)}, u32[]{:S(2)}, u32[]{:S(2)}) %collective-permute-start.2) | collective-permute-done | bytes 1048608 | tf_op jit(solution)/shard_map/ppermute | solution.py:20
  92.7 19.7 %collective-permute-done.3 = f32[64,4,8,128]{3,0,2,1:T(8,128)S(1)} collective-permute-done((f32[64,4,8,128]{3,0,2,1:T(8,128)S(1)}, f32[64,4,8,128]{3,0,2,1:T(8,128)S(1)}, u32[]{:S(2)}, u32[]{:S(2)}) %collective-permute-start.3) | collective-permute-done | bytes 1048608 | tf_op jit(solution)/shard_map/ppermute | solution.py:17
  112.4 5.2 fusion.15
  117.7 52.1 %all-gather.2.cloned.1.call-done = f32[256,4,8,128]{3,0,2,1:T(8,128)} async-done(((f32[64,4,8,128]{3,0,2,1:T(8,128)}), f32[256,4,8,128]{3,0,2,1:T(8,128)}) %all-gather.2.cloned.1.call-update) | async-done | bytes 4194320 | tf_op jit(solution)/shard_map/all_gather | solution.py:68
  169.8 7.1 convolution_bitcast_fusion
  176.9 5.3 copy.59
  182.3 581.9 %all-reduce.3.cloned.1.call-done = f32[64,256]{1,0:T(8,128)} async-done(((f32[64,256]{1,0:T(8,128)}), f32[64,256]{1,0:T(8,128)}) %all-reduce.3.cloned.1.call-update) | async-done | bytes 65552 | tf_op jit(solution)/shard_map/psum | solution.py:74
  765.0 41.7 %all_gather.7 = f32[256,256]{1,0:T(8,128)S(1)} all-gather(f32[64,256]{1,0:T(8,128)S(1)} %broadcast_multiply_fusion.1), channel_id=1, replica_groups=mesh['band'=4,'grid'=64] {'band'}, dimensions={0}, use_global_device_ids=true | all-gather | bytes 327680 | tf_op jit(solution)/shard_map/all_gather | solution.py:75
  806.9 11.7 %cholesky.50 = f32[128,128]{1,0:T(8,128)S(1)} custom-call(f32[128,128]{1,0:T(8,128)S(1)} %cholesky.118), custom_call_target="Cholesky" | custom-call | tf_op jit(solution)/shard_map/jit(cholesky)/cholesky | solution.py:58
  818.7 9.8 %custom-call.14 = f32[1,128,128]{1,2,0:T(8,128)S(1)} custom-call(f32[1,128,128]{2,1,0:T(8,128)S(1)} %get-tuple-element.38), custom_call_target="InvertDiagBlocksLowerTriangular" | custom-call | tf_op jit(solution)/shard_map/jit(cholesky)/cholesky | solution.py:58
  829.0 11.7 %cholesky.105 = f32[128,128]{1,0:T(8,128)S(1)} custom-call(f32[128,128]{1,0:T(8,128)S(1)} %convolution_subtract_fusion.1), custom_call_target="Cholesky" | custom-call | tf_op jit(solution)/shard_map/jit(cholesky)/cholesky | solution.py:58
  842.7 4.0 while.1
  843.5 1.3 bitcast_dynamic-update-slice_fusion.2
  845.4 1.3 bitcast_dynamic-update-slice_fusion.2
  846.7 19.7 %custom-call.15 = f32[2,128,128]{1,2,0:T(8,128)S(1)} custom-call(f32[2,128,128]{2,1,0:T(8,128)S(1)} %get-tuple-element.12), custom_call_target="InvertDiagBlocksLowerTriangular" | custom-call | tf_op jit(solution)/shard_map/triangular_solve | solution.py:60
  867.3 5.8 fusion
  873.1 1.6 copy.60
  (39 shorter events, 6.2 us)
Async XLA Ops:
  6.5 163.3 %all-gather.2.cloned.1.call-start = ((), (), s32[]{:S(2)}) async-start(), calls=%async_computation | async-start | bytes 5242880 | tf_op jit(solution)/shard_map/all_gather | solution.py:68
  8.4 47.9 %collective-permute-start.1 = (f32[64,4,8,128]{3,0,2,1:T(8,128)S(1)}, f32[64,4,8,128]{3,0,2,1:T(8,128)S(1)}, u32[]{:S(2)}, u32[]{:S(2)}) collective-permute-start(f32[64,4,8,128]{3,0,2,1:T(8,128)S(1)} %copy.42), channel_id=1, source_target_pairs={{0,1},{1,2},{2,3},{3,4},{4,5},{5,6},{6,7},{7,8},{8,9},{9,10},{10,1... | collective-permute-start | bytes 3145736 | tf_op jit(solution)/shard_map/ppermute | solution.py:17
  12.0 46.3 %collective-permute-start = (f32[64,4,8,128]{3,0,2,1:T(8,128)S(1)}, f32[64,4,8,128]{3,0,2,1:T(8,128)S(1)}, u32[]{:S(2)}, u32[]{:S(2)}) collective-permute-start(f32[64,4,8,128]{3,0,2,1:T(8,128)S(1)} %copy.42), channel_id=1, source_target_pairs={{1,0},{2,1},{3,2},{4,3},{5,4},{6,5},{7,6},{8,7},{9,8},{10,9},{11,1... | collective-permute-start | bytes 3145736 | tf_op jit(solution)/shard_map/ppermute | solution.py:20
  20.0 36.5 %copy-start = (f32[64,4,8,128]{3,2,1,0:T(8,128)S(1)}, f32[64,4,8,128]{3,2,1,0:T(8,128)}, u32[]{:S(2)}) copy-start(f32[64,4,8,128]{3,2,1,0:T(8,128)} %param.2) | copy-start | bytes 3145732
  56.4 2.0 copy-start.1
  62.9 29.8 %collective-permute-start.2 = (f32[64,4,8,128]{3,0,2,1:T(8,128)S(1)}, f32[64,4,8,128]{3,0,2,1:T(8,128)S(1)}, u32[]{:S(2)}, u32[]{:S(2)}) collective-permute-start(f32[64,4,8,128]{3,0,2,1:T(8,128)S(1)} %get-tuple-element.21), channel_id=1, source_target_pairs={{1,0},{2,1},{3,2},{4,3},{5,4},{6,5},{7,6},{8,7},{9,8},{10,9},{11,1... | collective-permute-start | bytes 3145736 | tf_op jit(solution)/shard_map/ppermute | solution.py:20
  70.6 41.8 %collective-permute-start.3 = (f32[64,4,8,128]{3,0,2,1:T(8,128)S(1)}, f32[64,4,8,128]{3,0,2,1:T(8,128)S(1)}, u32[]{:S(2)}, u32[]{:S(2)}) collective-permute-start(f32[64,4,8,128]{3,0,2,1:T(8,128)S(1)} %get-tuple-element.21), channel_id=1, source_target_pairs={{0,1},{1,2},{2,3},{3,4},{4,5},{5,6},{6,7},{7,8},{8,9},{9,10},{10,1... | collective-permute-start | bytes 3145736 | tf_op jit(solution)/shard_map/ppermute | solution.py:17
  117.6 646.6 %all-reduce.3.cloned.1.call-start = ((), (), s32[]{:S(2)}) async-start(), calls=%async_computation.1 | async-start | bytes 131072 | tf_op jit(solution)/shard_map/psum | solution.py:74
Sparse Core Ops, SparseCore 0:
  117.7 52.0 all-gather.1
  177.0 587.1 all-reduce.2
where the time goes:
time: 882 us
  waiting for transfers between devices  713 us (81%)
  other arithmetic  64.3 us (7%)
  blocking collectives  41.7 us (5%)
  starting transfers between devices  19.2 us (2%)
  between operations  14.8 us (2%)
  local copies, waits for them, and re-layouts  14.5 us (2%)
  matrix products  14.2 us (2%)
    psum x1, waiting for transfers between devices, body(): rows = lax.psum(partial_value, 'grid') / float(ncells)  582 us
    ppermute x2, waiting for transfers between devices, with_halo(): lax.ppermute(lax.slice_in_dim(block, block.shape[dim] - width, None, axis...  55.7 us
    all_gather x1, waiting for transfers between devices, body(): gathered = lax.all_gather(cur, 'band', axis=0, tiled=True)  52.1 us
    all_gather x1, blocking collectives, body(): margin = lax.all_gather(rows, 'band', axis=0, tiled=True)  41.7 us
    another operation x6, other arithmetic, lower_inverse(): factor = jnp.linalg.cholesky(margin)  33.9 us
    ppermute x2, waiting for transfers between devices, with_halo(): lax.ppermute(lax.slice_in_dim(block, 0, width, axis=dim), axis, backward)  22.8 us
    another operation x3, other arithmetic, lower_inverse(): lax.linalg.triangular_solve(factor, ident, left_side=True, lower=True)  19.7 us
  transfers between devices with their start and end apart: 6, of which 6 were waited for; matrix products, arithmetic and copies ran while one was open for 1% of the time, Pallas kernels for 0%

commit v1 on v0

v1 whole, which is shorter than its diff:
```python
import functools

import jax
import jax.numpy as jnp
from jax import lax
from jax.experimental import pallas as pl
from jax.experimental.pallas import tpu as pltpu
from jax.sharding import PartitionSpec as P

MESH = pl.DeviceIdType.MESH
HIGH = lax.Precision.HIGHEST
COEFS = (-205.0 / 72.0, 8.0 / 5.0, -1.0 / 5.0, 8.0 / 315.0, -1.0 / 560.0)
CENTER = 8.0
HALF = 4.0
SCALE = -0.5 / HALF
TAPS = tuple(SCALE * c for c in COEFS)
NCELLS = 256 * 8 * 128


def nt(a, b):
    return lax.dot_general(a, b, (((1,), (1,)), ((), ())), precision=HIGH, preferred_element_type=jnp.float32)


def nn(a, b):
    return lax.dot_general(a, b, (((1,), (0,)), ((), ())), precision=HIGH, preferred_element_type=jnp.float32)


def rotate_rows(c, k):
    k = k % 8
    return c if k == 0 else jnp.concatenate([c[k:], c[:k]], axis=0)


def stencil(read, t, coef):
    c = read(t)
    total = coef * c
    for k in range(1, 5):
        s = read(t - k) + read(t + k)
        s = s + (rotate_rows(c, k) + rotate_rows(c, -k))
        s = s + (pltpu.roll(c, k, 2) + pltpu.roll(c, 128 - k, 2))
        total = total + TAPS[k] * s
    return total


def main_kernel(orb_hbm, pot_ref, mt_out, gall, x_in, stage, vbuf, ybuf, abuf, fbuf, pots,
                mt, rx, zt, rz, ty, ry, zg,
                in_sem, pot_send, pot_recv, x_send, x_recv, h_send, h_recv, a_send, a_recv,
                rx_send, rx_recv, rz_send, rz_recv, ry_send, ry_recv, zg_send, zg_recv,
                mg_send, mg_recv, ga_send, ga_recv):
    b = lax.axis_index("band")
    g = lax.axis_index("grid")
    hi = lax.rem(g, 2)
    m = g // 2
    y = lax.rem(m, 4)
    z = m // 4
    p = hi * 4 + b
    up = lax.rem(m + 1, 32)
    down = lax.rem(m + 31, 32)

    def dev(bb, gg):
        return {"band": bb, "grid": gg}

    def copy(src, dst, ssem, rsem, target):
        return pltpu.make_async_remote_copy(src_ref=src, dst_ref=dst, send_sem=ssem, recv_sem=rsem,
                                            device_id=target, device_id_type=MESH)

    def await_bytes(ref, sem):
        pltpu.make_async_copy(ref, ref, sem).wait()

    def ring(i):
        q = lax.rem(p + i, 8)
        return q, dev(lax.rem(q, 4), m * 2 + q // 4)

    def yring(i):
        yy = lax.rem(y + i, 4)
        return yy, dev(b, (z * 4 + yy) * 2 + hi)

    def zring(i):
        zz = lax.rem(z + i, 8)
        return zz, dev(b, (zz * 4 + y) * 2 + hi)

    loads = []
    for c in range(4):
        for h in range(2):
            load = pltpu.make_async_copy(orb_hbm.at[pl.ds(h * 32 + c * 8, 8)], x_in.at[h, c], in_sem.at[h, c])
            load.start()
            loads.append(load)

    other = lax.rem(g + 63 + 2 * hi, 64)
    barrier = pltpu.get_barrier_semaphore()
    peers = [ring(i)[1] for i in range(1, 8)]
    peers += [dev(b, up * 2 + hi), dev(b, down * 2 + hi), dev(b, other)]
    peers += [yring(i)[1] for i in range(1, 4)]
    peers += [zring(i)[1] for i in range(1, 8)]
    for peer in peers:
        pl.semaphore_signal(barrier, inc=1, device_id=peer, device_id_type=MESH)
    pl.semaphore_wait(barrier, len(peers))

    pots[1 + hi] = pot_ref[...]
    side = m + 2 * hi - 1
    side = lax.rem(side + 32, 32)
    pot_copies = [
        copy(pots.at[1 + hi], pots.at[1 + hi], pot_send.at[0], pot_recv, dev(b, m * 2 + 1 - hi)),
        copy(pots.at[1 + hi], pots.at[3 - 3 * hi], pot_send.at[1], pot_recv, dev(b, side * 2)),
        copy(pots.at[1 + hi], pots.at[3 - 3 * hi], pot_send.at[2], pot_recv, dev(b, side * 2 + 1)),
    ]
    for item in pot_copies:
        item.start()

    far = lax.rem(b + 2, 4)
    x_copies = []
    for c in range(4):
        for h in range(2):
            loads[2 * c + h].wait()
            for plane in range(4):
                stage[h, c, plane] = jnp.swapaxes(x_in[h, c, :, plane], 0, 1)
            item = copy(stage.at[h, c], vbuf.at[c, pl.ds(8 + 4 * hi, 4)], x_send.at[h, c], x_recv.at[c], dev(far, m * 2 + h))
            item.start()
            x_copies.append(item)

    await_bytes(pots.at[pl.ds(0, 3)], pot_recv)
    for t in range(16):
        a = pots[t // 4, t % 4] * (1.0 / HALF) + (3.0 * TAPS[0] - CENTER / HALF)
        abuf[t] = jnp.broadcast_to(a[:, None, :], (8, 8, 128))

    h_copies = []
    for c in range(4):
        await_bytes(vbuf.at[c, pl.ds(8, 8)], x_recv.at[c])
        own = vbuf.at[c, pl.ds(8, 8)]
        pair = [
            copy(own, vbuf.at[c, pl.ds(0, 8)], h_send.at[c, 0], h_recv.at[c, 0], dev(b, up * 2 + hi)),
            copy(own, vbuf.at[c, pl.ds(16, 8)], h_send.at[c, 1], h_recv.at[c, 1], dev(b, down * 2 + hi)),
        ]
        for item in pair:
            item.start()
        h_copies.append(pair)

    a_copies = []
    row = far * 8 + hi * 4
    for c in range(4):
        for item in h_copies[c]:
            item.wait_recv()

        def first(t, _):
            ybuf[t] = stencil(lambda i: vbuf[c, i], t + 4, abuf[t])
            return 0

        def second(t, _):
            fbuf[c, t] = 2.0 * stencil(lambda i: ybuf[i], t + 4, abuf[t + 4]) - vbuf[c, t + 8]
            return 0

        lax.fori_loop(0, 16, first, 0)
        lax.fori_loop(0, 8, second, 0)
        for i in range(1, 8):
            q, target = ring(i)
            item = copy(fbuf.at[c, q], gall.at[lax.rem(q, 4), row + c], a_send.at[c, i - 1], a_recv, target)
            item.start()
            a_copies.append(item)
        pltpu.make_async_copy(fbuf.at[c, p], gall.at[b, row + c], a_recv).start()
    await_bytes(gall.at[b], a_recv)

    sib = b + 1 - 2 * lax.rem(b, 2)
    to_sib = copy(gall.at[b], gall.at[b], ga_send.at[0], ga_recv.at[0], dev(sib, g))
    to_far = copy(gall.at[b], gall.at[b], ga_send.at[1], ga_recv.at[1], dev(far, g))
    relay = copy(gall.at[far], gall.at[far], ga_send.at[2], ga_recv.at[2], dev(sib, g))
    to_sib.start()

    acc = None
    for pair in range(4):
        a = jnp.concatenate([gall[b, :, 2 * pair].reshape(256, 128), gall[b, :, 2 * pair + 1].reshape(256, 128)], axis=1)
        term = nt(a, a)
        acc = term if acc is None else acc + term
    acc = acc * (1.0 / NCELLS)
    for half in range(2):
        mt[:, half * 4:half * 4 + 4] = acc[:, half * 128:half * 128 + 128].reshape(8, 4, 8, 128)

    sends = []
    for i in range(1, 8):
        q, target = ring(i)
        item = copy(mt.at[q], rx.at[i - 1], rx_send.at[i - 1], rx_recv, target)
        item.start()
        sends.append(item)
    await_bytes(rx, rx_recv)
    total = mt[p]
    for i in range(7):
        total = total + rx[i]
    zt[...] = total
    for i in range(1, 8):
        q, target = zring(i)
        item = copy(zt.at[q], rz.at[i - 1], rz_send.at[i - 1], rz_recv, target)
        item.start()
        sends.append(item)
    await_bytes(rz, rz_recv)
    tile = zt[z]
    for i in range(7):
        tile = tile + rz[i]
    ry[y] = tile
    for i in range(1, 4):
        q, target = yring(i)
        item = copy(ry.at[y], ry.at[y], ry_send.at[i - 1], ry_recv, target)
        item.start()
        sends.append(item)
    await_bytes(ty, ry_recv)
    zg[z] = ry[0] + ry[1] + ry[2] + ry[3]
    for i in range(1, 8):
        q, target = zring(i)
        item = copy(zg.at[z], zg.at[z], zg_send.at[i - 1], zg_recv, target)
        item.start()
        sends.append(item)
    await_bytes(rz, zg_recv)
    mt_out[p] = zg[...]
    for i in range(1, 8):
        q, target = ring(i)
        item = copy(zg, mt_out.at[p], mg_send.at[i - 1], mg_recv, target)
        item.start()
        sends.append(item)
    await_bytes(rx, mg_recv)

    to_far.start()
    to_far.wait_recv()
    relay.start()
    to_sib.wait_recv()
    relay.wait_recv()

    for item in pot_copies + x_copies + a_copies + sends + [to_sib, to_far, relay]:
        item.wait_send()
    for pair in h_copies:
        for item in pair:
            item.wait_send()


def inverse_factor(block):
    lane = lax.broadcasted_iota(jnp.int32, (8, 128), 1)
    sub = lax.broadcasted_iota(jnp.int32, (8, 128), 0)
    groups = [block[8 * i:8 * i + 8] for i in range(16)]
    for n in range(16):
        panel = groups[n]
        base = 8 * n
        d = [[None] * 8 for _ in range(8)]
        for j in range(8):
            column = jnp.broadcast_to(panel[:, base + j:base + j + 1], (8, 128))
            for i in range(j, 8):
                d[i][j] = jnp.broadcast_to(column[i:i + 1], (8, 128))
        inside = (lane >= base) & (lane < base + 8)
        masked = jnp.where(inside, jnp.where(lane == base + sub, 1.0, 0.0), panel)
        rows = [jnp.broadcast_to(masked[k:k + 1], (8, 128)) for k in range(8)]
        for j in range(8):
            r = lax.rsqrt(d[j][j])
            for i in range(j + 1, 8):
                d[i][j] = d[i][j] * r
            rows[j] = rows[j] * r
            for i in range(j + 1, 8):
                rows[i] = rows[i] - d[i][j] * rows[j]
                for k in range(j + 1, i + 1):
                    d[i][k] = d[i][k] - d[i][j] * d[k][j]
        out = rows[0]
        for k in range(1, 8):
            out = jnp.where(sub == k, rows[k], out)
        groups[n] = out
        for i in range(n + 1, 16):
            cur = jnp.where(inside, 0.0, groups[i])
            where = sub + 8 * i
            for j in range(8):
                cur = cur - jnp.take_along_axis(rows[j], where, axis=1) * rows[j]
            groups[i] = cur
    return jnp.concatenate([jnp.where(lane <= sub + 8 * i, groups[i], 0.0) for i in range(16)], axis=0)


def tail_kernel(mt, gall, out, w):
    b = lax.axis_index("band")

    def block(i, j):
        return mt[4 * i:4 * i + 4, 4 * j:4 * j + 4].reshape(128, 128)

    w11 = inverse_factor(block(0, 0))
    l21 = nt(block(1, 0), w11)
    w22 = inverse_factor(block(1, 1) - nt(l21, l21))
    w[0:128, 0:128] = w11
    w[0:128, 128:256] = jnp.zeros((128, 128), jnp.float32)
    w[128:256, 0:128] = -nn(w22, nn(l21, w11))
    w[128:256, 128:256] = w22
    mine = w[pl.ds(pl.multiple_of(b * 64, 64), 64), :]

    def plane(t, _):
        for pair in range(4):
            f = jnp.concatenate([gall[t, :, 2 * pair].reshape(256, 128), gall[t, :, 2 * pair + 1].reshape(256, 128)], axis=1)
            res = nn(mine, f)
            out[:, t, 2 * pair, :] = res[:, :128]
            out[:, t, 2 * pair + 1, :] = res[:, 128:]
        return 0

    lax.fori_loop(0, 4, plane, 0)


def body(orbitals, potential):
    f32 = jnp.float32
    dma = pltpu.SemaphoreType.DMA
    vmem = functools.partial(pl.BlockSpec, memory_space=pltpu.VMEM)
    mt, gall = pl.pallas_call(
        main_kernel,
        out_shape=(jax.ShapeDtypeStruct((8, 8, 8, 128), f32), jax.ShapeDtypeStruct((4, 32, 8, 8, 128), f32)),
        in_specs=[pl.BlockSpec(memory_space=pl.ANY), vmem()],
        out_specs=(vmem(), vmem()),
        scratch_shapes=[
            pltpu.VMEM((2, 4, 8, 4, 8, 128), f32),
            pltpu.VMEM((2, 4, 4, 8, 8, 128), f32),
            pltpu.VMEM((4, 24, 8, 8, 128), f32),
            pltpu.VMEM((16, 8, 8, 128), f32),
            pltpu.VMEM((16, 8, 8, 128), f32),
            pltpu.VMEM((4, 8, 8, 8, 128), f32),
            pltpu.VMEM((4, 4, 8, 128), f32),
            pltpu.VMEM((8, 8, 8, 128), f32),
            pltpu.VMEM((7, 8, 8, 128), f32),
            pltpu.VMEM((8, 8, 128), f32),
            pltpu.VMEM((7, 8, 128), f32),
            pltpu.VMEM((3, 8, 128), f32),
            pltpu.VMEM((4, 8, 128), f32),
            pltpu.VMEM((8, 8, 128), f32),
            dma((2, 4)),
            dma((3,)), dma,
            dma((2, 4)), dma((4,)),
            dma((4, 2)), dma((4, 2)),
            dma((4, 7)), dma,
            dma((7,)), dma,
            dma((7,)), dma,
            dma((3,)), dma,
            dma((7,)), dma,
            dma((7,)), dma,
            dma((3,)), dma((3,)),
        ],
        compiler_params=pltpu.CompilerParams(collective_id=0, has_side_effects=True, vmem_limit_bytes=40 * 2**20),
    )(orbitals, potential)
    return pl.pallas_call(
        tail_kernel,
        out_shape=jax.ShapeDtypeStruct(orbitals.shape, f32),
        in_specs=[vmem(), vmem()],
        out_specs=vmem(),
        scratch_shapes=[pltpu.VMEM((256, 256), f32)],
        compiler_params=pltpu.CompilerParams(vmem_limit_bytes=40 * 2**20),
    )(mt, gall)


def solution(mesh):
    return jax.shard_map(
        body,
        mesh=mesh,
        in_specs=(P("band", "grid", None, None), P("grid", None, None)),
        out_specs=P("band", "grid", None, None),
        check_vma=False,
    )
```

time: 882 us -> 116 us (0.13)
  waiting for transfers between devices: 713 us -> 0 us
  Pallas kernels: 0 us -> 114 us
  other arithmetic: 64.3 us -> 0 us
  blocking collectives: 41.7 us -> 0 us
  starting transfers between devices: 19.2 us -> 0 us
  between operations: 14.8 us -> 0.01 us
  matrix products: 14.2 us -> 0 us
  local copies, waits for them, and re-layouts: 14.5 us -> 1.94 us
    psum x1 -> x0, waiting for transfers between devices: 582 us -> none  [body(): rows = lax.psum(partial_value, 'grid') / float(ncells)]
    pallas_call x0 -> x2, Pallas kernels: none -> 114 us  [the longest x1 101 us: body(): pl.pallas_call(main_kernel, out_shape=(jax.ShapeDtypeStruct((8, 8, 8, 128...]
    ppermute x4 -> x0, waiting for transfers between devices: 78.5 us -> none  [the longest x2 55.7 us: with_halo(): lax.ppermute(lax.slice_in_dim(block, block.shape[dim] - width, None, axis...]
    another operation x9 -> x0, other arithmetic: 53.7 us -> none  [the longest x6 33.9 us: lower_inverse(): factor = jnp.linalg.cholesky(margin)]
    all_gather x1 -> x0, waiting for transfers between devices: 52.1 us -> none  [body(): gathered = lax.all_gather(cur, 'band', axis=0, tiled=True)]
    all_gather x1 -> x0, blocking collectives: 41.7 us -> none  [body(): margin = lax.all_gather(rows, 'band', axis=0, tiled=True)]
    ppermute x4 -> x0, starting transfers between devices: 19.2 us -> none  [the longest x2 15.5 us: with_halo(): lax.ppermute(lax.slice_in_dim(block, 0, width, axis=dim), axis, backward)]
    dot_general x2 -> x0, matrix products: 12.9 us -> none  [the longest x1 7.08 us: body(): jnp.dot(own, whole.T, precision=lax.Precision.HIGHEST, preferred_element_...]
  transfers between devices with their start and end apart: 6 -> 0, of which waited for: 6 -> 0; matrix products, arithmetic and copies ran while one was open for 1% -> 0% of each run, Pallas kernels for 0% -> 0%
where the time goes in v1:
time: 116 us
  Pallas kernels  114 us (98%)
  local copies, waits for them, and re-layouts  1.94 us (2%)
    pallas_call x1, Pallas kernels, body(): pl.pallas_call(main_kernel, out_shape=(jax.ShapeDtypeStruct((8, 8, 8, 128...  101 us
    pallas_call x1, Pallas kernels, body(): pl.pallas_call(tail_kernel, out_shape=jax.ShapeDtypeStruct(orbitals.shape...  12.9 us

profile of v1, /device:TPU:1, one launch (start us, length us, event | category | flops | bytes accessed | tf_op | source)
XLA Modules:
  0.0 115.6 jit_solution(16010160829006699106)
XLA Ops:
  0.0 0.0 copy-start
  0.0 1.2 %copy-done = f32[64,4,8,128]{3,2,1,0:T(8,128)S(1)} copy-done((f32[64,4,8,128]{3,2,1,0:T(8,128)S(1)}, f32[64,4,8,128]{3,2,1,0:T(8,128)}, u32[]{:S(2)}) %copy-start) | copy-done | bytes 1048600
  1.2 0.0 copy-start.1
  1.2 0.7 copy-done.1
  1.9 100.8 %shard_map.28 = (f32[8,8,8,128]{3,2,1,0:T(8,128)S(1)}, f32[4,32,8,8,128]{4,3,2,1,0:T(8,128)S(1)}) custom-call(f32[64,4,8,128]{3,2,1,0:T(8,128)S(1)} %copy-done, f32[4,8,128]{2,1,0:T(8,128)S(1)} %copy-done.1), custom_call_target="tpu_custom_call" | custom-call | tf_op jit(solution)/shard_map/pallas_call | solution.py:298
  102.7 12.9 %shard_map.29 = f32[64,4,8,128]{3,2,1,0:T(8,128)} custom-call(f32[8,8,8,128]{3,2,1,0:T(8,128)S(1)} %get-tuple-element.7.mt, f32[4,32,8,8,128]{4,3,2,1,0:T(8,128)S(1)} %get-tuple-element.8.gall), custom_call_target="tpu_custom_call" | custom-call | tf_op jit(solution)/shard_map/pallas_call | solution.py:332
Async XLA Ops:
  0.0 1.2 %copy-start = (f32[64,4,8,128]{3,2,1,0:T(8,128)S(1)}, f32[64,4,8,128]{3,2,1,0:T(8,128)}, u32[]{:S(2)}) copy-start(f32[64,4,8,128]{3,2,1,0:T(8,128)} %orb_hbm.1) | copy-start | bytes 3145732
  1.2 0.7 copy-start.1

commit v2 on v1

--- a/solution.py
+++ b/solution.py
@@ -41,11 +41,11 @@
     return total
 
 
-def main_kernel(orb_hbm, pot_ref, mt_out, gall, x_in, stage, vbuf, ybuf, abuf, fbuf, pots,
-                mt, rx, zt, rz, ty, ry, zg,
-                in_sem, pot_send, pot_recv, x_send, x_recv, h_send, h_recv, a_send, a_recv,
-                rx_send, rx_recv, rz_send, rz_recv, ry_send, ry_recv, zg_send, zg_recv,
-                mg_send, mg_recv, ga_send, ga_recv):
+def main_kernel(orb_hbm, pot_hbm, w_out, gall, x_in, stage, vbuf, ybuf, abuf, fbuf, pots,
+                mt, pair_in, half_sum, layer_in, zsum, mg,
+                in_sem, pot_in, pot_send, pot_recv, x_send, x_recv, h_send, h_recv, a_send, a_recv,
+                pair_send, pair_recv, layer_send, layer_recv, z_send, z_recv,
+                spread_send, spread_recv, back_send, back_recv, ga_send, ga_recv):
     b = lax.axis_index("band")
     g = lax.axis_index("grid")
     hi = lax.rem(g, 2)
@@ -53,6 +53,8 @@
     y = lax.rem(m, 4)
     z = m // 4
     p = hi * 4 + b
+    core = lax.rem(b, 2)
+    chip = (y * 2 + hi) * 2 + b // 2
     up = lax.rem(m + 1, 32)
     down = lax.rem(m + 31, 32)
 
@@ -70,14 +72,16 @@
         q = lax.rem(p + i, 8)
         return q, dev(lax.rem(q, 4), m * 2 + q // 4)
 
-    def yring(i):
-        yy = lax.rem(y + i, 4)
-        return yy, dev(b, (z * 4 + yy) * 2 + hi)
+    def layer(i):
+        q = lax.rem(chip + i, 16)
+        return q, dev(lax.rem(q, 2) * 2 + core, z * 8 + q // 2)
 
     def zring(i):
         zz = lax.rem(z + i, 8)
-        return zz, dev(b, (zz * 4 + y) * 2 + hi)
-
+        return zz, dev(b, zz * 8 + y * 2 + hi)
+
+    pot_load = pltpu.make_async_copy(pot_hbm, pots.at[1 + hi], pot_in)
+    pot_load.start()
     loads = []
     for c in range(4):
         for h in range(2):
@@ -89,15 +93,45 @@
     barrier = pltpu.get_barrier_semaphore()
     peers = [ring(i)[1] for i in range(1, 8)]
     peers += [dev(b, up * 2 + hi), dev(b, down * 2 + hi), dev(b, other)]
-    peers += [yring(i)[1] for i in range(1, 4)]
+    peers += [layer(i)[1] for i in range(1, 16)]
     peers += [zring(i)[1] for i in range(1, 8)]
     for peer in peers:
         pl.semaphore_signal(barrier, inc=1, device_id=peer, device_id_type=MESH)
+
+    far = lax.rem(b + 2, 4)
+    sib = b + 1 - 2 * core
+    x_copies = []
+
+    def turn(c):
+        for h in range(2):
+            loads[2 * c + h].wait()
+            for plane in range(4):
+                stage[h, c, plane] = jnp.swapaxes(x_in[h, c, :, plane], 0, 1)
+
+    def send_x(c):
+        for h in range(2):
+            item = copy(stage.at[h, c], vbuf.at[c, pl.ds(8 + 4 * hi, 4)], x_send.at[h, c], x_recv.at[c], dev(far, m * 2 + h))
+            item.start()
+            x_copies.append(item)
+
+    h_copies = {}
+
+    def send_halo(c):
+        await_bytes(vbuf.at[c, pl.ds(8, 8)], x_recv.at[c])
+        own = vbuf.at[c, pl.ds(8, 8)]
+        h_copies[c] = [
+            copy(own, vbuf.at[c, pl.ds(0, 8)], h_send.at[c, 0], h_recv.at[c, 0], dev(b, up * 2 + hi)),
+            copy(own, vbuf.at[c, pl.ds(16, 8)], h_send.at[c, 1], h_recv.at[c, 1], dev(b, down * 2 + hi)),
+        ]
+        for item in h_copies[c]:
+            item.start()
+
+    turn(0)
     pl.semaphore_wait(barrier, len(peers))
-
-    pots[1 + hi] = pot_ref[...]
-    side = m + 2 * hi - 1
-    side = lax.rem(side + 32, 32)
+    send_x(0)
+
+    pot_load.wait()
+    side = lax.rem(m + 2 * hi + 31, 32)
     pot_copies = [
         copy(pots.at[1 + hi], pots.at[1 + hi], pot_send.at[0], pot_recv, dev(b, m * 2 + 1 - hi)),
         copy(pots.at[1 + hi], pots.at[3 - 3 * hi], pot_send.at[1], pot_recv, dev(b, side * 2)),
@@ -105,40 +139,26 @@
     ]
     for item in pot_copies:
         item.start()
-
-    far = lax.rem(b + 2, 4)
-    x_copies = []
-    for c in range(4):
-        for h in range(2):
-            loads[2 * c + h].wait()
-            for plane in range(4):
-                stage[h, c, plane] = jnp.swapaxes(x_in[h, c, :, plane], 0, 1)
-            item = copy(stage.at[h, c], vbuf.at[c, pl.ds(8 + 4 * hi, 4)], x_send.at[h, c], x_recv.at[c], dev(far, m * 2 + h))
-            item.start()
-            x_copies.append(item)
-
+    turn(1)
+    send_x(1)
+    turn(2)
+    turn(3)
+    send_halo(0)
+    send_x(2)
     await_bytes(pots.at[pl.ds(0, 3)], pot_recv)
     for t in range(16):
         a = pots[t // 4, t % 4] * (1.0 / HALF) + (3.0 * TAPS[0] - CENTER / HALF)
         abuf[t] = jnp.broadcast_to(a[:, None, :], (8, 8, 128))
-
-    h_copies = []
-    for c in range(4):
-        await_bytes(vbuf.at[c, pl.ds(8, 8)], x_recv.at[c])
-        own = vbuf.at[c, pl.ds(8, 8)]
-        pair = [
-            copy(own, vbuf.at[c, pl.ds(0, 8)], h_send.at[c, 0], h_recv.at[c, 0], dev(b, up * 2 + hi)),
-            copy(own, vbuf.at[c, pl.ds(16, 8)], h_send.at[c, 1], h_recv.at[c, 1], dev(b, down * 2 + hi)),
-        ]
-        for item in pair:
-            item.start()
-        h_copies.append(pair)
+    send_halo(1)
+    send_x(3)
 
     a_copies = []
     row = far * 8 + hi * 4
     for c in range(4):
         for item in h_copies[c]:
             item.wait_recv()
+        if c + 2 < 4:
+            send_halo(c + 2)
 
         def first(t, _):
             ybuf[t] = stencil(lambda i: vbuf[c, i], t + 4, abuf[t])
@@ -158,11 +178,9 @@
         pltpu.make_async_copy(fbuf.at[c, p], gall.at[b, row + c], a_recv).start()
     await_bytes(gall.at[b], a_recv)
 
-    sib = b + 1 - 2 * lax.rem(b, 2)
     to_sib = copy(gall.at[b], gall.at[b], ga_send.at[0], ga_recv.at[0], dev(sib, g))
     to_far = copy(gall.at[b], gall.at[b], ga_send.at[1], ga_recv.at[1], dev(far, g))
     relay = copy(gall.at[far], gall.at[far], ga_send.at[2], ga_recv.at[2], dev(sib, g))
-    to_sib.start()
 
     acc = None
     for pair in range(4):
@@ -171,60 +189,63 @@
         acc = term if acc is None else acc + term
     acc = acc * (1.0 / NCELLS)
     for half in range(2):
-        mt[:, half * 4:half * 4 + 4] = acc[:, half * 128:half * 128 + 128].reshape(8, 4, 8, 128)
+        mt[half] = acc[:, half * 128:half * 128 + 128].reshape(16, 2, 8, 128)
 
     sends = []
-    for i in range(1, 8):
-        q, target = ring(i)
-        item = copy(mt.at[q], rx.at[i - 1], rx_send.at[i - 1], rx_recv, target)
+    item = copy(mt.at[1 - core], pair_in, pair_send, pair_recv, dev(sib, g))
+    item.start()
+    sends.append(item)
+    item.wait_recv()
+    half_sum[...] = mt[core] + pair_in[...]
+    for i in range(1, 16):
+        q, target = layer(i)
+        item = copy(half_sum.at[q], layer_in.at[i - 1], layer_send.at[i - 1], layer_recv, target)
         item.start()
         sends.append(item)
-    await_bytes(rx, rx_recv)
-    total = mt[p]
-    for i in range(7):
-        total = total + rx[i]
-    zt[...] = total
+    to_far.start()
+    to_sib.start()
+    await_bytes(layer_in, layer_recv)
+    total = half_sum[chip]
+    for i in range(15):
+        total = total + layer_in[i]
+    zsum[z] = total
     for i in range(1, 8):
         q, target = zring(i)
-        item = copy(zt.at[q], rz.at[i - 1], rz_send.at[i - 1], rz_recv, target)
+        item = copy(zsum.at[z], zsum.at[z], z_send.at[i - 1], z_recv, target)
         item.start()
         sends.append(item)
-    await_bytes(rz, rz_recv)
-    tile = zt[z]
-    for i in range(7):
-        tile = tile + rz[i]
-    ry[y] = tile
-    for i in range(1, 4):
-        q, target = yring(i)
-        item = copy(ry.at[y], ry.at[y], ry_send.at[i - 1], ry_recv, target)
+    await_bytes(zsum.at[pl.ds(0, 7)], z_recv)
+    total = zsum[0]
+    for i in range(1, 8):
+        total = total + zsum[i]
+    mg[core, chip] = total
+    for i in range(1, 16):
+        q, target = layer(i)
+        item = copy(mg.at[core, chip], mg.at[core, chip], spread_send.at[i - 1], spread_recv, target)
         item.start()
         sends.append(item)
-    await_bytes(ty, ry_recv)
-    zg[z] = ry[0] + ry[1] + ry[2] + ry[3]
-    for i in range(1, 8):
-        q, target = zring(i)
-        item = copy(zg.at[z], zg.at[z], zg_send.at[i - 1], zg_recv, target)
-        item.start()
-        sends.append(item)
-    await_bytes(rz, zg_recv)
-    mt_out[p] = zg[...]
-    for i in range(1, 8):
-        q, target = ring(i)
-        item = copy(zg, mt_out.at[p], mg_send.at[i - 1], mg_recv, target)
-        item.start()
-        sends.append(item)
-    await_bytes(rx, mg_recv)
-
-    to_far.start()
+    await_bytes(layer_in, spread_recv)
+    item = copy(mg.at[core], mg.at[core], back_send, back_recv, dev(sib, g))
+    item.start()
+    sends.append(item)
+    item.wait_recv()
+
+    w11 = inverse_factor(mg[0, 0:8].reshape(128, 128))
     to_far.wait_recv()
     relay.start()
+    l21 = nt(mg[0, 8:16].reshape(128, 128), w11)
+    w22 = inverse_factor(mg[1, 8:16].reshape(128, 128) - nt(l21, l21))
+    w_out[0:128, 0:128] = w11
+    w_out[0:128, 128:256] = jnp.zeros((128, 128), jnp.float32)
+    w_out[128:256, 0:128] = -nn(w22, nn(l21, w11))
+    w_out[128:256, 128:256] = w22
     to_sib.wait_recv()
     relay.wait_recv()
 
     for item in pot_copies + x_copies + a_copies + sends + [to_sib, to_far, relay]:
         item.wait_send()
-    for pair in h_copies:
-        for item in pair:
+    for c in range(4):
+        for item in h_copies[c]:
             item.wait_send()
 
 
@@ -265,19 +286,8 @@
     return jnp.concatenate([jnp.where(lane <= sub + 8 * i, groups[i], 0.0) for i in range(16)], axis=0)
 
 
-def tail_kernel(mt, gall, out, w):
+def tail_kernel(w, gall, out):
     b = lax.axis_index("band")
-
-    def block(i, j):
-        return mt[4 * i:4 * i + 4, 4 * j:4 * j + 4].reshape(128, 128)
-
-    w11 = inverse_factor(block(0, 0))
-    l21 = nt(block(1, 0), w11)
-    w22 = inverse_factor(block(1, 1) - nt(l21, l21))
-    w[0:128, 0:128] = w11
-    w[0:128, 128:256] = jnp.zeros((128, 128), jnp.float32)
-    w[128:256, 0:128] = -nn(w22, nn(l21, w11))
-    w[128:256, 128:256] = w22
     mine = w[pl.ds(pl.multiple_of(b * 64, 64), 64), :]
 
     def plane(t, _):
@@ -295,10 +305,11 @@
     f32 = jnp.float32
     dma = pltpu.SemaphoreType.DMA
     vmem = functools.partial(pl.BlockSpec, memory_space=pltpu.VMEM)
-    mt, gall = pl.pallas_call(
+    hbm = functools.partial(pl.BlockSpec, memory_space=pltpu.HBM)
+    w, gall = pl.pallas_call(
         main_kernel,
-        out_shape=(jax.ShapeDtypeStruct((8, 8, 8, 128), f32), jax.ShapeDtypeStruct((4, 32, 8, 8, 128), f32)),
-        in_specs=[pl.BlockSpec(memory_space=pl.ANY), vmem()],
+        out_shape=(jax.ShapeDtypeStruct((256, 256), f32), jax.ShapeDtypeStruct((4, 32, 8, 8, 128), f32)),
+        in_specs=[hbm(), hbm()],
         out_specs=(vmem(), vmem()),
         scratch_shapes=[
             pltpu.VMEM((2, 4, 8, 4, 8, 128), f32),
@@ -308,23 +319,22 @@
             pltpu.VMEM((16, 8, 8, 128), f32),
             pltpu.VMEM((4, 8, 8, 8, 128), f32),
             pltpu.VMEM((4, 4, 8, 128), f32),
-            pltpu.VMEM((8, 8, 8, 128), f32),
-            pltpu.VMEM((7, 8, 8, 128), f32),
-            pltpu.VMEM((8, 8, 128), f32),
-            pltpu.VMEM((7, 8, 128), f32),
-            pltpu.VMEM((3, 8, 128), f32),
-            pltpu.VMEM((4, 8, 128), f32),
-            pltpu.VMEM((8, 8, 128), f32),
-            dma((2, 4)),
+            pltpu.VMEM((2, 16, 2, 8, 128), f32),
+            pltpu.VMEM((16, 2, 8, 128), f32),
+            pltpu.VMEM((16, 2, 8, 128), f32),
+            pltpu.VMEM((15, 2, 8, 128), f32),
+            pltpu.VMEM((8, 2, 8, 128), f32),
+            pltpu.VMEM((2, 16, 2, 8, 128), f32),
+            dma((2, 4)), dma,
             dma((3,)), dma,
             dma((2, 4)), dma((4,)),
             dma((4, 2)), dma((4, 2)),
             dma((4, 7)), dma,
+            dma, dma,
+            dma((15,)), dma,
             dma((7,)), dma,
-            dma((7,)), dma,
-            dma((3,)), dma,
-            dma((7,)), dma,
-            dma((7,)), dma,
+            dma((15,)), dma,
+            dma, dma,
             dma((3,)), dma((3,)),
         ],
         compiler_params=pltpu.CompilerParams(collective_id=0, has_side_effects=True, vmem_limit_bytes=40 * 2**20),
@@ -334,9 +344,8 @@
         out_shape=jax.ShapeDtypeStruct(orbitals.shape, f32),
         in_specs=[vmem(), vmem()],
         out_specs=vmem(),
-        scratch_shapes=[pltpu.VMEM((256, 256), f32)],
         compiler_params=pltpu.CompilerParams(vmem_limit_bytes=40 * 2**20),
-    )(mt, gall)
+    )(w, gall)
 
 
 def solution(mesh):

time: 116 us -> 98.4 us (0.85)
  Pallas kernels: 114 us -> 96.3 us
    pallas_call x1, Pallas kernels: 12.9 us -> 4.15 us  [body(): pl.pallas_call(tail_kernel, out_shape=jax.ShapeDtypeStruct(orbitals.shape...]
    pallas_call x1, Pallas kernels: 101 us -> 92.1 us  [body(): pl.pallas_call(main_kernel, out_shape=(jax.ShapeDtypeStruct((256, 256), f...]
where the time goes in v2:
time: 98.4 us; the launch traced here: 98.3 us
  Pallas kernels  96.3 us (98%)
  local copies, waits for them, and re-layouts  1.94 us (2%)
    pallas_call x1, Pallas kernels, body(): pl.pallas_call(main_kernel, out_shape=(jax.ShapeDtypeStruct((256, 256), f...  92.1 us
    pallas_call x1, Pallas kernels, body(): pl.pallas_call(tail_kernel, out_shape=jax.ShapeDtypeStruct(orbitals.shape...  4.15 us

profile of v2, /device:TPU:1, one launch (start us, length us, event | category | flops | bytes accessed | tf_op | source)
XLA Modules:
  0.0 98.3 jit_solution(9462155236256157411)
XLA Ops:
  0.0 0.0 copy-start
  0.0 1.2 %copy-done = f32[64,4,8,128]{3,2,1,0:T(8,128)S(1)} copy-done((f32[64,4,8,128]{3,2,1,0:T(8,128)S(1)}, f32[64,4,8,128]{3,2,1,0:T(8,128)}, u32[]{:S(2)}) %copy-start) | copy-done | bytes 1048600
  1.2 0.0 copy-start.1
  1.2 0.7 copy-done.1
  1.9 92.1 %shard_map.28 = (f32[256,256]{1,0:T(8,128)S(1)}, f32[4,32,8,8,128]{4,3,2,1,0:T(8,128)S(1)}) custom-call(f32[64,4,8,128]{3,2,1,0:T(8,128)S(1)} %copy-done, f32[4,8,128]{2,1,0:T(8,128)S(1)} %copy-done.1), custom_call_target="tpu_custom_call" | custom-call | tf_op jit(solution)/shard_map/pallas_call | solution.py:309
  94.1 4.2 %shard_map.29 = f32[64,4,8,128]{3,2,1,0:T(8,128)} custom-call(f32[256,256]{1,0:T(8,128)S(1)} %get-tuple-element.7.w, f32[4,32,8,8,128]{4,3,2,1,0:T(8,128)S(1)} %get-tuple-element.8.gall), custom_call_target="tpu_custom_call" | custom-call | tf_op jit(solution)/shard_map/pallas_call | solution.py:342
Async XLA Ops:
  0.0 1.2 %copy-start = (f32[64,4,8,128]{3,2,1,0:T(8,128)S(1)}, f32[64,4,8,128]{3,2,1,0:T(8,128)}, u32[]{:S(2)}) copy-start(f32[64,4,8,128]{3,2,1,0:T(8,128)} %orb_hbm.1) | copy-start | bytes 3145732
  1.2 0.7 copy-start.1

commit v3 on v2

--- a/solution.py
+++ b/solution.py
@@ -15,6 +15,7 @@
 SCALE = -0.5 / HALF
 TAPS = tuple(SCALE * c for c in COEFS)
 NCELLS = 256 * 8 * 128
+GROUP = 4
 
 
 def nt(a, b):
@@ -26,26 +27,34 @@
 
 
 def rotate_rows(c, k):
-    k = k % 8
-    return c if k == 0 else jnp.concatenate([c[k:], c[:k]], axis=0)
-
-
-def stencil(read, t, coef):
-    c = read(t)
-    total = coef * c
+    return jnp.concatenate([c[:, k:], c[:, :k]], axis=1)
+
+
+def circulant():
+    i = lax.broadcasted_iota(jnp.int32, (128, 128), 0)
+    j = lax.broadcasted_iota(jnp.int32, (128, 128), 1)
+    apart = lax.rem(i - j + 128, 128)
+    total = jnp.zeros((128, 128), jnp.float32)
     for k in range(1, 5):
-        s = read(t - k) + read(t + k)
-        s = s + (rotate_rows(c, k) + rotate_rows(c, -k))
-        s = s + (pltpu.roll(c, k, 2) + pltpu.roll(c, 128 - k, 2))
+        total = jnp.where((apart == k) | (apart == 128 - k), TAPS[k], total)
+    return total
+
+
+def stencil(read, coef, along_z):
+    c = read(0)
+    total = coef * c + nn(c.reshape(GROUP * 64, 128), along_z).reshape(GROUP, 8, 8, 128)
+    for k in range(1, 5):
+        s = read(-k) + read(k)
+        s = s + (rotate_rows(c, k) + rotate_rows(c, 8 - k))
         total = total + TAPS[k] * s
     return total
 
 
-def main_kernel(orb_hbm, pot_hbm, w_out, gall, x_in, stage, vbuf, ybuf, abuf, fbuf, pots,
+def kernel(orb_hbm, pot_hbm, out_hbm, gall, x_in, stage, vbuf, ybuf, abuf, fbuf, zmat, pots, w, res,
                 mt, pair_in, half_sum, layer_in, zsum, mg,
                 in_sem, pot_in, pot_send, pot_recv, x_send, x_recv, h_send, h_recv, a_send, a_recv,
                 pair_send, pair_recv, layer_send, layer_recv, z_send, z_recv,
-                spread_send, spread_recv, back_send, back_recv, ga_send, ga_recv):
+                spread_send, spread_recv, back_send, back_recv, ga_send, ga_recv, out_sem):
     b = lax.axis_index("band")
     g = lax.axis_index("grid")
     hi = lax.rem(g, 2)
@@ -127,6 +136,7 @@
             item.start()
 
     turn(0)
+    zmat[...] = circulant()
     pl.semaphore_wait(barrier, len(peers))
     send_x(0)
 
@@ -152,39 +162,61 @@
     send_halo(1)
     send_x(3)
 
+    to_sib, to_far, relay = [], [], []
+
+    def send_plane(c):
+        to_far.append(copy(gall.at[b, c], gall.at[b, c], ga_send.at[1, c], ga_recv.at[1, c], dev(far, g)))
+        to_sib.append(copy(gall.at[b, c], gall.at[b, c], ga_send.at[0, c], ga_recv.at[0, c], dev(sib, g)))
+        to_far[c].start()
+        to_sib[c].start()
+
+    def send_relay(c):
+        to_far[c].wait_recv()
+        relay.append(copy(gall.at[far, c], gall.at[far, c], ga_send.at[2, c], ga_recv.at[2, c], dev(sib, g)))
+        relay[c].start()
+
     a_copies = []
-    row = far * 8 + hi * 4
+    row = far * 2 + hi
     for c in range(4):
         for item in h_copies[c]:
             item.wait_recv()
         if c + 2 < 4:
             send_halo(c + 2)
 
-        def first(t, _):
-            ybuf[t] = stencil(lambda i: vbuf[c, i], t + 4, abuf[t])
+        def first(i, _):
+            t = i * GROUP
+            ybuf[pl.ds(t, GROUP)] = stencil(lambda k: vbuf[c, pl.ds(t + 4 + k, GROUP)], abuf[pl.ds(t, GROUP)], zmat[...])
             return 0
 
-        def second(t, _):
-            fbuf[c, t] = 2.0 * stencil(lambda i: ybuf[i], t + 4, abuf[t + 4]) - vbuf[c, t + 8]
+        def second(i, _):
+            t = i * GROUP
+            step = stencil(lambda k: ybuf[pl.ds(t + 4 + k, GROUP)], abuf[pl.ds(t + 4, GROUP)], zmat[...])
+            fbuf[c, pl.ds(t, GROUP)] = 2.0 * step - vbuf[c, pl.ds(t + 8, GROUP)]
             return 0
 
-        lax.fori_loop(0, 16, first, 0)
-        lax.fori_loop(0, 8, second, 0)
+        lax.fori_loop(0, 16 // GROUP, first, 0, unroll=2)
+        lax.fori_loop(0, 8 // GROUP, second, 0, unroll=2)
         for i in range(1, 8):
             q, target = ring(i)
-            item = copy(fbuf.at[c, q], gall.at[lax.rem(q, 4), row + c], a_send.at[c, i - 1], a_recv, target)
+            item = copy(fbuf.at[c, q], gall.at[lax.rem(q, 4), c, row], a_send.at[c, i - 1], a_recv.at[c], target)
             item.start()
             a_copies.append(item)
-        pltpu.make_async_copy(fbuf.at[c, p], gall.at[b, row + c], a_recv).start()
-    await_bytes(gall.at[b], a_recv)
-
-    to_sib = copy(gall.at[b], gall.at[b], ga_send.at[0], ga_recv.at[0], dev(sib, g))
-    to_far = copy(gall.at[b], gall.at[b], ga_send.at[1], ga_recv.at[1], dev(far, g))
-    relay = copy(gall.at[far], gall.at[far], ga_send.at[2], ga_recv.at[2], dev(sib, g))
+        pltpu.make_async_copy(fbuf.at[c, p], gall.at[b, c, row], a_recv.at[c]).start()
+        if c >= 1:
+            await_bytes(gall.at[b, c - 1], a_recv.at[c - 1])
+        if c in (1, 2):
+            send_plane(c - 1)
+    send_relay(0)
+    await_bytes(gall.at[b, 3], a_recv.at[3])
+
+    def orbitals_of(t, pair):
+        return jnp.concatenate([
+            jnp.concatenate([gall[t, c, slot, row] for slot in range(8) for c in range(4)], axis=0)
+            for row in (2 * pair, 2 * pair + 1)], axis=1)
 
     acc = None
     for pair in range(4):
-        a = jnp.concatenate([gall[b, :, 2 * pair].reshape(256, 128), gall[b, :, 2 * pair + 1].reshape(256, 128)], axis=1)
+        a = orbitals_of(b, pair)
         term = nt(a, a)
         acc = term if acc is None else acc + term
     acc = acc * (1.0 / NCELLS)
@@ -202,8 +234,8 @@
         item = copy(half_sum.at[q], layer_in.at[i - 1], layer_send.at[i - 1], layer_recv, target)
         item.start()
         sends.append(item)
-    to_far.start()
-    to_sib.start()
+    send_plane(2)
+    send_plane(3)
     await_bytes(layer_in, layer_recv)
     total = half_sum[chip]
     for i in range(15):
@@ -230,23 +262,40 @@
     sends.append(item)
     item.wait_recv()
 
+    send_relay(1)
     w11 = inverse_factor(mg[0, 0:8].reshape(128, 128))
-    to_far.wait_recv()
-    relay.start()
+    send_relay(2)
+    send_relay(3)
     l21 = nt(mg[0, 8:16].reshape(128, 128), w11)
     w22 = inverse_factor(mg[1, 8:16].reshape(128, 128) - nt(l21, l21))
-    w_out[0:128, 0:128] = w11
-    w_out[0:128, 128:256] = jnp.zeros((128, 128), jnp.float32)
-    w_out[128:256, 0:128] = -nn(w22, nn(l21, w11))
-    w_out[128:256, 128:256] = w22
-    to_sib.wait_recv()
-    relay.wait_recv()
-
-    for item in pot_copies + x_copies + a_copies + sends + [to_sib, to_far, relay]:
+    w[0:128, 0:128] = w11
+    w[0:128, 128:256] = jnp.zeros((128, 128), jnp.float32)
+    w[128:256, 0:128] = -nn(w22, nn(l21, w11))
+    w[128:256, 128:256] = w22
+
+    mine = w[pl.ds(pl.multiple_of(b * 64, 64), 64), :]
+    outs = []
+    for n, t in enumerate((b, sib, far, lax.rem(sib + 2, 4))):
+        for c in range(4):
+            if n == 1:
+                to_sib[c].wait_recv()
+            if n == 3:
+                relay[c].wait_recv()
+        for pair in range(4):
+            block = nn(mine, orbitals_of(t, pair))
+            res[t, :, 2 * pair, :] = block[:, :128]
+            res[t, :, 2 * pair + 1, :] = block[:, 128:]
+        item = pltpu.make_async_copy(res.at[t], out_hbm.at[:, t], out_sem.at[n])
+        item.start()
+        outs.append(item)
+
+    for item in pot_copies + x_copies + a_copies + sends + to_sib + to_far + relay:
         item.wait_send()
     for c in range(4):
         for item in h_copies[c]:
             item.wait_send()
+    for item in outs:
+        item.wait()
 
 
 def inverse_factor(block):
@@ -286,39 +335,27 @@
     return jnp.concatenate([jnp.where(lane <= sub + 8 * i, groups[i], 0.0) for i in range(16)], axis=0)
 
 
-def tail_kernel(w, gall, out):
-    b = lax.axis_index("band")
-    mine = w[pl.ds(pl.multiple_of(b * 64, 64), 64), :]
-
-    def plane(t, _):
-        for pair in range(4):
-            f = jnp.concatenate([gall[t, :, 2 * pair].reshape(256, 128), gall[t, :, 2 * pair + 1].reshape(256, 128)], axis=1)
-            res = nn(mine, f)
-            out[:, t, 2 * pair, :] = res[:, :128]
-            out[:, t, 2 * pair + 1, :] = res[:, 128:]
-        return 0
-
-    lax.fori_loop(0, 4, plane, 0)
-
-
 def body(orbitals, potential):
     f32 = jnp.float32
     dma = pltpu.SemaphoreType.DMA
-    vmem = functools.partial(pl.BlockSpec, memory_space=pltpu.VMEM)
-    hbm = functools.partial(pl.BlockSpec, memory_space=pltpu.HBM)
-    w, gall = pl.pallas_call(
-        main_kernel,
-        out_shape=(jax.ShapeDtypeStruct((256, 256), f32), jax.ShapeDtypeStruct((4, 32, 8, 8, 128), f32)),
+    hbm = functools.partial(pl.BlockSpec, memory_space=pl.ANY)
+    return pl.pallas_call(
+        kernel,
+        out_shape=jax.ShapeDtypeStruct(orbitals.shape, f32),
         in_specs=[hbm(), hbm()],
-        out_specs=(vmem(), vmem()),
+        out_specs=hbm(),
         scratch_shapes=[
+            pltpu.VMEM((4, 4, 8, 8, 8, 128), f32),
             pltpu.VMEM((2, 4, 8, 4, 8, 128), f32),
             pltpu.VMEM((2, 4, 4, 8, 8, 128), f32),
             pltpu.VMEM((4, 24, 8, 8, 128), f32),
             pltpu.VMEM((16, 8, 8, 128), f32),
             pltpu.VMEM((16, 8, 8, 128), f32),
             pltpu.VMEM((4, 8, 8, 8, 128), f32),
+            pltpu.VMEM((128, 128), f32),
             pltpu.VMEM((4, 4, 8, 128), f32),
+            pltpu.VMEM((256, 256), f32),
+            pltpu.VMEM((4, 64, 8, 128), f32),
             pltpu.VMEM((2, 16, 2, 8, 128), f32),
             pltpu.VMEM((16, 2, 8, 128), f32),
             pltpu.VMEM((16, 2, 8, 128), f32),
@@ -329,23 +366,16 @@
             dma((3,)), dma,
             dma((2, 4)), dma((4,)),
             dma((4, 2)), dma((4, 2)),
-            dma((4, 7)), dma,
+            dma((4, 7)), dma((4,)),
             dma, dma,
             dma((15,)), dma,
             dma((7,)), dma,
             dma((15,)), dma,
             dma, dma,
-            dma((3,)), dma((3,)),
+            dma((3, 4)), dma((3, 4)), dma((4,)),
         ],
-        compiler_params=pltpu.CompilerParams(collective_id=0, has_side_effects=True, vmem_limit_bytes=40 * 2**20),
+        compiler_params=pltpu.CompilerParams(collective_id=0, has_side_effects=True, vmem_limit_bytes=60 * 2**20),
     )(orbitals, potential)
-    return pl.pallas_call(
-        tail_kernel,
-        out_shape=jax.ShapeDtypeStruct(orbitals.shape, f32),
-        in_specs=[vmem(), vmem()],
-        out_specs=vmem(),
-        compiler_params=pltpu.CompilerParams(vmem_limit_bytes=40 * 2**20),
-    )(w, gall)
 
 
 def solution(mesh):

time: 98.4 us -> 91.8 us (0.933)
  Pallas kernels: 96.3 us -> 89.4 us
    pallas_call x2 -> x1, Pallas kernels: 96.3 us -> 89.4 us  [body(): pl.pallas_call(kernel, out_shape=jax.ShapeDtypeStruct(orbitals.shape, f32...]
    unnamed x4 -> x1, local copies, waits for them, and re-layouts: 1.94 us -> 2.26 us
where the time goes in v3:
time: 91.8 us; the launch traced here: 91.7 us
  Pallas kernels  89.4 us (97%)
  local copies, waits for them, and re-layouts  2.26 us (2%)
    pallas_call x1, Pallas kernels, body(): pl.pallas_call(kernel, out_shape=jax.ShapeDtypeStruct(orbitals.shape, f32...  89.4 us
    unnamed x1, local copies, waits for them, and re-layouts  2.26 us

profile of v3, /device:TPU:1, one launch (start us, length us, event | category | flops | bytes accessed | tf_op | source)
XLA Modules:
  0.0 91.7 jit_solution(9119933921625868211)
XLA Ops:
  0.0 89.4 %shard_map.28 = f32[64,4,8,128]{3,2,1,0:T(8,128)} custom-call(f32[64,4,8,128]{3,2,1,0:T(8,128)} %orb_hbm.1, f32[4,8,128]{2,1,0:T(8,128)} %pot_hbm.1), custom_call_target="tpu_custom_call" | custom-call | tf_op jit(solution)/shard_map/pallas_call | solution.py:342
  89.4 2.3 %copy.4 = f32[64,4,8,128]{3,2,1,0:T(8,128)} copy(f32[64,4,8,128]{3,2,1,0:T(8,128)} %shard_map.28) | data formatting | bytes 2097152

commit v4 on v3

--- a/solution.py
+++ b/solution.py
@@ -50,11 +50,17 @@
     return total
 
 
-def kernel(orb_hbm, pot_hbm, out_hbm, gall, x_in, stage, vbuf, ybuf, abuf, fbuf, zmat, pots, w, res,
+def orbitals_of(gall, t, pair):
+    return jnp.concatenate([
+        jnp.concatenate([gall[t, c, slot, row] for slot in range(8) for c in range(4)], axis=0)
+        for row in (2 * pair, 2 * pair + 1)], axis=1)
+
+
+def main_kernel(orb_hbm, pot_hbm, w, gall, x_in, stage, vbuf, ybuf, abuf, fbuf, zmat, pots,
                 mt, pair_in, half_sum, layer_in, zsum, mg,
                 in_sem, pot_in, pot_send, pot_recv, x_send, x_recv, h_send, h_recv, a_send, a_recv,
                 pair_send, pair_recv, layer_send, layer_recv, z_send, z_recv,
-                spread_send, spread_recv, back_send, back_recv, ga_send, ga_recv, out_sem):
+                spread_send, spread_recv, back_send, back_recv, ga_send, ga_recv):
     b = lax.axis_index("band")
     g = lax.axis_index("grid")
     hi = lax.rem(g, 2)
@@ -204,19 +210,11 @@
         pltpu.make_async_copy(fbuf.at[c, p], gall.at[b, c, row], a_recv.at[c]).start()
         if c >= 1:
             await_bytes(gall.at[b, c - 1], a_recv.at[c - 1])
-        if c in (1, 2):
-            send_plane(c - 1)
-    send_relay(0)
     await_bytes(gall.at[b, 3], a_recv.at[3])
-
-    def orbitals_of(t, pair):
-        return jnp.concatenate([
-            jnp.concatenate([gall[t, c, slot, row] for slot in range(8) for c in range(4)], axis=0)
-            for row in (2 * pair, 2 * pair + 1)], axis=1)
 
     acc = None
     for pair in range(4):
-        a = orbitals_of(b, pair)
+        a = orbitals_of(gall, b, pair)
         term = nt(a, a)
         acc = term if acc is None else acc + term
     acc = acc * (1.0 / NCELLS)
@@ -234,8 +232,8 @@
         item = copy(half_sum.at[q], layer_in.at[i - 1], layer_send.at[i - 1], layer_recv, target)
         item.start()
         sends.append(item)
-    send_plane(2)
-    send_plane(3)
+    send_plane(0)
+    send_plane(1)
     await_bytes(layer_in, layer_recv)
     total = half_sum[chip]
     for i in range(15):
@@ -256,46 +254,34 @@
         item = copy(mg.at[core, chip], mg.at[core, chip], spread_send.at[i - 1], spread_recv, target)
         item.start()
         sends.append(item)
+    send_plane(2)
+    send_plane(3)
     await_bytes(layer_in, spread_recv)
     item = copy(mg.at[core], mg.at[core], back_send, back_recv, dev(sib, g))
     item.start()
     sends.append(item)
     item.wait_recv()
 
+    send_relay(0)
     send_relay(1)
     w11 = inverse_factor(mg[0, 0:8].reshape(128, 128))
     send_relay(2)
-    send_relay(3)
     l21 = nt(mg[0, 8:16].reshape(128, 128), w11)
     w22 = inverse_factor(mg[1, 8:16].reshape(128, 128) - nt(l21, l21))
     w[0:128, 0:128] = w11
     w[0:128, 128:256] = jnp.zeros((128, 128), jnp.float32)
     w[128:256, 0:128] = -nn(w22, nn(l21, w11))
     w[128:256, 128:256] = w22
-
-    mine = w[pl.ds(pl.multiple_of(b * 64, 64), 64), :]
-    outs = []
-    for n, t in enumerate((b, sib, far, lax.rem(sib + 2, 4))):
-        for c in range(4):
-            if n == 1:
-                to_sib[c].wait_recv()
-            if n == 3:
-                relay[c].wait_recv()
-        for pair in range(4):
-            block = nn(mine, orbitals_of(t, pair))
-            res[t, :, 2 * pair, :] = block[:, :128]
-            res[t, :, 2 * pair + 1, :] = block[:, 128:]
-        item = pltpu.make_async_copy(res.at[t], out_hbm.at[:, t], out_sem.at[n])
-        item.start()
-        outs.append(item)
-
+    send_relay(3)
+
+    for c in range(4):
+        to_sib[c].wait_recv()
+        relay[c].wait_recv()
     for item in pot_copies + x_copies + a_copies + sends + to_sib + to_far + relay:
         item.wait_send()
     for c in range(4):
         for item in h_copies[c]:
             item.wait_send()
-    for item in outs:
-        item.wait()
 
 
 def inverse_factor(block):
@@ -335,17 +321,35 @@
     return jnp.concatenate([jnp.where(lane <= sub + 8 * i, groups[i], 0.0) for i in range(16)], axis=0)
 
 
+def product_kernel(w, gall, out_hbm, res, out_sem):
+    b = lax.axis_index("band")
+    mine = w[pl.ds(pl.multiple_of(b * 64, 64), 64), :]
+    outs = []
+    for t in range(4):
+        for pair in range(4):
+            block = nn(mine, orbitals_of(gall, t, pair))
+            res[t, :, 2 * pair, :] = block[:, :128]
+            res[t, :, 2 * pair + 1, :] = block[:, 128:]
+        item = pltpu.make_async_copy(res.at[t], out_hbm.at[:, t], out_sem.at[t])
+        item.start()
+        outs.append(item)
+    for item in outs:
+        item.wait()
+
+
 def body(orbitals, potential):
     f32 = jnp.float32
     dma = pltpu.SemaphoreType.DMA
-    hbm = functools.partial(pl.BlockSpec, memory_space=pl.ANY)
-    return pl.pallas_call(
-        kernel,
-        out_shape=jax.ShapeDtypeStruct(orbitals.shape, f32),
-        in_specs=[hbm(), hbm()],
-        out_specs=hbm(),
+    anywhere = functools.partial(pl.BlockSpec, memory_space=pl.ANY)
+    vmem = functools.partial(pl.BlockSpec, memory_space=pltpu.VMEM)
+    orbitals = pltpu.with_memory_space_constraint(orbitals, pltpu.HBM)
+    potential = pltpu.with_memory_space_constraint(potential, pltpu.HBM)
+    w, gall = pl.pallas_call(
+        main_kernel,
+        out_shape=(jax.ShapeDtypeStruct((256, 256), f32), jax.ShapeDtypeStruct((4, 4, 8, 8, 8, 128), f32)),
+        in_specs=[anywhere(), anywhere()],
+        out_specs=(vmem(), vmem()),
         scratch_shapes=[
-            pltpu.VMEM((4, 4, 8, 8, 8, 128), f32),
             pltpu.VMEM((2, 4, 8, 4, 8, 128), f32),
             pltpu.VMEM((2, 4, 4, 8, 8, 128), f32),
             pltpu.VMEM((4, 24, 8, 8, 128), f32),
@@ -354,8 +358,6 @@
             pltpu.VMEM((4, 8, 8, 8, 128), f32),
             pltpu.VMEM((128, 128), f32),
             pltpu.VMEM((4, 4, 8, 128), f32),
-            pltpu.VMEM((256, 256), f32),
-            pltpu.VMEM((4, 64, 8, 128), f32),
             pltpu.VMEM((2, 16, 2, 8, 128), f32),
             pltpu.VMEM((16, 2, 8, 128), f32),
             pltpu.VMEM((16, 2, 8, 128), f32),
@@ -372,10 +374,18 @@
             dma((7,)), dma,
             dma((15,)), dma,
             dma, dma,
-            dma((3, 4)), dma((3, 4)), dma((4,)),
+            dma((3, 4)), dma((3, 4)),
         ],
-        compiler_params=pltpu.CompilerParams(collective_id=0, has_side_effects=True, vmem_limit_bytes=60 * 2**20),
+        compiler_params=pltpu.CompilerParams(collective_id=0, has_side_effects=True, vmem_limit_bytes=40 * 2**20),
     )(orbitals, potential)
+    return pl.pallas_call(
+        product_kernel,
+        out_shape=jax.ShapeDtypeStruct(orbitals.shape, f32),
+        in_specs=[vmem(), vmem()],
+        out_specs=anywhere(),
+        scratch_shapes=[pltpu.VMEM((4, 64, 8, 128), f32), dma((4,))],
+        compiler_params=pltpu.CompilerParams(vmem_limit_bytes=40 * 2**20),
+    )(w, gall)
 
 
 def solution(mesh):

time: 91.8 us -> 82.2 us (0.90)
  Pallas kernels: 89.4 us -> 81.9 us
  local copies, waits for them, and re-layouts: 2.26 us -> 0 us
    pallas_call x1 -> x2, Pallas kernels: 89.4 us -> 81.9 us  [the longest x1 78.5 us: body(): pl.pallas_call(main_kernel, out_shape=(jax.ShapeDtypeStruct((256, 256), f...]
    unnamed x1 -> x0, local copies, waits for them, and re-layouts: 2.26 us -> none
where the time goes in v4:
time: 82.2 us; the launch traced here: 82.1 us
  Pallas kernels  81.9 us (100%)
    pallas_call x1, Pallas kernels, body(): pl.pallas_call(main_kernel, out_shape=(jax.ShapeDtypeStruct((256, 256), f...  78.5 us
    pallas_call x1, Pallas kernels, body(): pl.pallas_call(product_kernel, out_shape=jax.ShapeDtypeStruct(orbitals.sh...  3.36 us

profile of v4, /device:TPU:1, one launch (start us, length us, event | category | flops | bytes accessed | tf_op | source)
XLA Modules:
  0.0 82.1 jit_solution(12335685332012305955)
XLA Ops:
  0.0 78.5 %shard_map.28 = (f32[256,256]{1,0:T(8,128)S(1)}, f32[4,4,8,8,8,128]{5,4,3,2,1,0:T(8,128)S(1)}) custom-call(f32[64,4,8,128]{3,2,1,0:T(8,128)} %orb_hbm.1, f32[4,8,128]{2,1,0:T(8,128)} %pot_hbm.1), custom_call_target="tpu_custom_call" | custom-call | tf_op jit(solution)/shard_map/pallas_call | solution.py:347
  78.5 3.4 %shard_map.29 = f32[64,4,8,128]{3,2,1,0:T(8,128)} custom-call(f32[256,256]{1,0:T(8,128)S(1)} %get-tuple-element.7.w, f32[4,4,8,8,8,128]{5,4,3,2,1,0:T(8,128)S(1)} %get-tuple-element.8.gall), custom_call_target="tpu_custom_call" | custom-call | tf_op jit(solution)/shard_map/pallas_call | solution.py:381

commit v5 on v4

--- a/solution.py
+++ b/solution.py
@@ -17,6 +17,8 @@
 NCELLS = 256 * 8 * 128
 GROUP = 4
 
+SPLIT = (0, 1, 1, 4)
+
 
 def nt(a, b):
     return lax.dot_general(a, b, (((1,), (1,)), ((), ())), precision=HIGH, preferred_element_type=jnp.float32)
@@ -58,7 +60,7 @@
 
 def main_kernel(orb_hbm, pot_hbm, w, gall, x_in, stage, vbuf, ybuf, abuf, fbuf, zmat, pots,
                 mt, pair_in, half_sum, layer_in, zsum, mg,
-                in_sem, pot_in, pot_send, pot_recv, x_send, x_recv, h_send, h_recv, a_send, a_recv,
+                in_sem, pot_in, pot_send, pot_recv, x_send, x_recv, first_send, first_recv, first_out, h_send, h_recv, a_send, a_recv,
                 pair_send, pair_recv, layer_send, layer_recv, z_send, z_recv,
                 spread_send, spread_recv, back_send, back_recv, ga_send, ga_recv):
     b = lax.axis_index("band")
@@ -95,6 +97,15 @@
         zz = lax.rem(z + i, 8)
         return zz, dev(b, zz * 8 + y * 2 + hi)
 
+    other = lax.rem(g + 63 + 2 * hi, 64)
+    barrier = pltpu.get_barrier_semaphore()
+    peers = [zring(i)[1] for i in (4, 3, 5, 2, 6, 1, 7)]
+    peers += [layer(i)[1] for i in (10, 9, 11, 6, 14, 8, 2, 7, 13, 5, 3, 1, 4, 12, 15)]
+    peers += [ring(i)[1] for i in range(1, 8)]
+    peers += [dev(b, up * 2 + hi), dev(b, down * 2 + hi), dev(b, other)]
+    for peer in peers:
+        pl.semaphore_signal(barrier, inc=1, device_id=peer, device_id_type=MESH)
+
     pot_load = pltpu.make_async_copy(pot_hbm, pots.at[1 + hi], pot_in)
     pot_load.start()
     loads = []
@@ -104,15 +115,6 @@
             load.start()
             loads.append(load)
 
-    other = lax.rem(g + 63 + 2 * hi, 64)
-    barrier = pltpu.get_barrier_semaphore()
-    peers = [ring(i)[1] for i in range(1, 8)]
-    peers += [dev(b, up * 2 + hi), dev(b, down * 2 + hi), dev(b, other)]
-    peers += [layer(i)[1] for i in range(1, 16)]
-    peers += [zring(i)[1] for i in range(1, 8)]
-    for peer in peers:
-        pl.semaphore_signal(barrier, inc=1, device_id=peer, device_id_type=MESH)
-
     far = lax.rem(b + 2, 4)
     sib = b + 1 - 2 * core
     x_copies = []
@@ -125,6 +127,12 @@
 
     def send_x(c):
         for h in range(2):
+            if c == 0:
+                for t in range(4):
+                    item = copy(stage.at[h, 0, t], vbuf.at[0, 8 + 4 * hi + t], first_send.at[h, t], first_recv.at[t], dev(far, m * 2 + h))
+                    item.start()
+                    x_copies.append(item)
+                continue
             item = copy(stage.at[h, c], vbuf.at[c, pl.ds(8 + 4 * hi, 4)], x_send.at[h, c], x_recv.at[c], dev(far, m * 2 + h))
             item.start()
             x_copies.append(item)
@@ -132,6 +140,18 @@
     h_copies = {}
 
     def send_halo(c):
+        if c == 0:
+            h_copies[0] = []
+            for t in range(4):
+                await_bytes(vbuf.at[0, pl.ds(8, 2)], first_recv.at[t])
+                for side in range(2):
+                    for k in range(2):
+                        at = 16 * side + 4 * k + t
+                        item = copy(vbuf.at[0, 8 + 4 * k + t], vbuf.at[0, at], first_out.at[t, k, side],
+                                    h_recv.at[0, side], dev(b, (down if side else up) * 2 + hi))
+                        item.start()
+                        h_copies[0].append(item)
+            return
         await_bytes(vbuf.at[c, pl.ds(8, 8)], x_recv.at[c])
         own = vbuf.at[c, pl.ds(8, 8)]
         h_copies[c] = [
@@ -170,22 +190,29 @@
 
     to_sib, to_far, relay = [], [], []
 
-    def send_plane(c):
-        to_far.append(copy(gall.at[b, c], gall.at[b, c], ga_send.at[1, c], ga_recv.at[1, c], dev(far, g)))
-        to_sib.append(copy(gall.at[b, c], gall.at[b, c], ga_send.at[0, c], ga_recv.at[0, c], dev(sib, g)))
-        to_far[c].start()
-        to_sib[c].start()
-
-    def send_relay(c):
-        to_far[c].wait_recv()
-        relay.append(copy(gall.at[far, c], gall.at[far, c], ga_send.at[2, c], ga_recv.at[2, c], dev(sib, g)))
-        relay[c].start()
+    def piece(plane, k):
+        return gall.at[plane, k // 2, pl.ds(4 * (k % 2), 4)]
+
+    def gather(lo, hi_):
+        for k in range(lo, hi_):
+            own = piece(b, k)
+            to_far.append(copy(own, own, ga_send.at[1, k], ga_recv.at[1, k], dev(far, g)))
+            to_sib.append(copy(own, own, ga_send.at[0, k], ga_recv.at[0, k], dev(sib, g)))
+            to_far[k].start()
+            to_sib[k].start()
+
+    def pass_on(lo, hi_):
+        for k in range(lo, hi_):
+            to_far[k].wait_recv()
+            theirs = piece(far, k)
+            relay.append(copy(theirs, theirs, ga_send.at[2, k], ga_recv.at[2, k], dev(sib, g)))
+            relay[k].start()
 
     a_copies = []
     row = far * 2 + hi
     for c in range(4):
-        for item in h_copies[c]:
-            item.wait_recv()
+        await_bytes(vbuf.at[c, pl.ds(0, 8)], h_recv.at[c, 0])
+        await_bytes(vbuf.at[c, pl.ds(16, 8)], h_recv.at[c, 1])
         if c + 2 < 4:
             send_halo(c + 2)
 
@@ -194,24 +221,25 @@
             ybuf[pl.ds(t, GROUP)] = stencil(lambda k: vbuf[c, pl.ds(t + 4 + k, GROUP)], abuf[pl.ds(t, GROUP)], zmat[...])
             return 0
 
-        def second(i, _):
-            t = i * GROUP
-            step = stencil(lambda k: ybuf[pl.ds(t + 4 + k, GROUP)], abuf[pl.ds(t + 4, GROUP)], zmat[...])
-            fbuf[c, pl.ds(t, GROUP)] = 2.0 * step - vbuf[c, pl.ds(t + 8, GROUP)]
-            return 0
-
         lax.fori_loop(0, 16 // GROUP, first, 0, unroll=2)
-        lax.fori_loop(0, 8 // GROUP, second, 0, unroll=2)
-        for i in range(1, 8):
-            q, target = ring(i)
-            item = copy(fbuf.at[c, q], gall.at[lax.rem(q, 4), c, row], a_send.at[c, i - 1], a_recv.at[c], target)
-            item.start()
-            a_copies.append(item)
+        for n in range(2):
+            half = 1 - hi if n == 0 else hi
+            t = half * 4
+            step = stencil(lambda k: ybuf[pl.ds(t + 4 + k, 4)], abuf[pl.ds(t + 4, 4)], zmat[...])
+            fbuf[c, pl.ds(t, 4)] = 2.0 * step - vbuf[c, pl.ds(t + 8, 4)]
+            for i in range(n, 4):
+                bb = lax.rem(b + i, 4)
+                item = copy(fbuf.at[c, t + bb], gall.at[bb, c, row], a_send.at[c, 4 * n + i], a_recv.at[c], dev(bb, m * 2 + half))
+                item.start()
+                a_copies.append(item)
         pltpu.make_async_copy(fbuf.at[c, p], gall.at[b, c, row], a_recv.at[c]).start()
         if c >= 1:
             await_bytes(gall.at[b, c - 1], a_recv.at[c - 1])
+        if c in (1, 2):
+            gather(SPLIT[c - 1], SPLIT[c])
     await_bytes(gall.at[b, 3], a_recv.at[3])
 
+    sends = []
     acc = None
     for pair in range(4):
         a = orbitals_of(gall, b, pair)
@@ -220,20 +248,18 @@
     acc = acc * (1.0 / NCELLS)
     for half in range(2):
         mt[half] = acc[:, half * 128:half * 128 + 128].reshape(16, 2, 8, 128)
-
-    sends = []
     item = copy(mt.at[1 - core], pair_in, pair_send, pair_recv, dev(sib, g))
     item.start()
     sends.append(item)
-    item.wait_recv()
+
+    sends[0].wait_recv()
     half_sum[...] = mt[core] + pair_in[...]
     for i in range(1, 16):
         q, target = layer(i)
         item = copy(half_sum.at[q], layer_in.at[i - 1], layer_send.at[i - 1], layer_recv, target)
         item.start()
         sends.append(item)
-    send_plane(0)
-    send_plane(1)
+    gather(SPLIT[2], SPLIT[3])
     await_bytes(layer_in, layer_recv)
     total = half_sum[chip]
     for i in range(15):
@@ -254,29 +280,27 @@
         item = copy(mg.at[core, chip], mg.at[core, chip], spread_send.at[i - 1], spread_recv, target)
         item.start()
         sends.append(item)
-    send_plane(2)
-    send_plane(3)
+    gather(SPLIT[3], 8)
     await_bytes(layer_in, spread_recv)
     item = copy(mg.at[core], mg.at[core], back_send, back_recv, dev(sib, g))
     item.start()
     sends.append(item)
     item.wait_recv()
 
-    send_relay(0)
-    send_relay(1)
+    pass_on(0, SPLIT[3])
     w11 = inverse_factor(mg[0, 0:8].reshape(128, 128))
-    send_relay(2)
+    pass_on(SPLIT[3], 6)
     l21 = nt(mg[0, 8:16].reshape(128, 128), w11)
     w22 = inverse_factor(mg[1, 8:16].reshape(128, 128) - nt(l21, l21))
     w[0:128, 0:128] = w11
     w[0:128, 128:256] = jnp.zeros((128, 128), jnp.float32)
     w[128:256, 0:128] = -nn(w22, nn(l21, w11))
     w[128:256, 128:256] = w22
-    send_relay(3)
-
-    for c in range(4):
-        to_sib[c].wait_recv()
-        relay[c].wait_recv()
+    pass_on(6, 8)
+
+    for k in range(8):
+        to_sib[k].wait_recv()
+        relay[k].wait_recv()
     for item in pot_copies + x_copies + a_copies + sends + to_sib + to_far + relay:
         item.wait_send()
     for c in range(4):
@@ -327,7 +351,7 @@
     outs = []
     for t in range(4):
         for pair in range(4):
-            block = nn(mine, orbitals_of(gall, t, pair))
+            block = lax.dot_general(mine, orbitals_of(gall, t, pair), (((1,), (0,)), ((), ())), precision=lax.Precision.HIGH, preferred_element_type=jnp.float32)
             res[t, :, 2 * pair, :] = block[:, :128]
             res[t, :, 2 * pair + 1, :] = block[:, 128:]
         item = pltpu.make_async_copy(res.at[t], out_hbm.at[:, t], out_sem.at[t])
@@ -367,14 +391,15 @@
             dma((2, 4)), dma,
             dma((3,)), dma,
             dma((2, 4)), dma((4,)),
+            dma((2, 4)), dma((4,)), dma((4, 2, 2)),
             dma((4, 2)), dma((4, 2)),
-            dma((4, 7)), dma((4,)),
+            dma((4, 8)), dma((4,)),
             dma, dma,
             dma((15,)), dma,
             dma((7,)), dma,
             dma((15,)), dma,
             dma, dma,
-            dma((3, 4)), dma((3, 4)),
+            dma((3, 8)), dma((3, 8)),
         ],
         compiler_params=pltpu.CompilerParams(collective_id=0, has_side_effects=True, vmem_limit_bytes=40 * 2**20),
     )(orbitals, potential)

time: 82.2 us -> 77.9 us (0.948)
  Pallas kernels: 81.9 us -> 77.6 us
    pallas_call x1, Pallas kernels: 78.5 us -> 75.2 us  [body(): pl.pallas_call(main_kernel, out_shape=(jax.ShapeDtypeStruct((256, 256), f...]
    pallas_call x1, Pallas kernels: 3.36 us -> 2.41 us  [body(): pl.pallas_call(product_kernel, out_shape=jax.ShapeDtypeStruct(orbitals.sh...]
where the time goes in v5:
time: 77.9 us; the launch traced here: 77.8 us
  Pallas kernels  77.6 us (100%)
    pallas_call x1, Pallas kernels, body(): pl.pallas_call(main_kernel, out_shape=(jax.ShapeDtypeStruct((256, 256), f...  75.2 us
    pallas_call x1, Pallas kernels, body(): pl.pallas_call(product_kernel, out_shape=jax.ShapeDtypeStruct(orbitals.sh...  2.41 us

profile of v5, /device:TPU:1, one launch (start us, length us, event | category | flops | bytes accessed | tf_op | source)
XLA Modules:
  0.0 77.8 jit_solution(5964126928895183419)
XLA Ops:
  0.0 75.2 %shard_map.28 = (f32[256,256]{1,0:T(8,128)S(1)}, f32[4,4,8,8,8,128]{5,4,3,2,1,0:T(8,128)S(1)}) custom-call(f32[64,4,8,128]{3,2,1,0:T(8,128)} %orb_hbm.1, f32[4,8,128]{2,1,0:T(8,128)} %pot_hbm.1), custom_call_target="tpu_custom_call" | custom-call | tf_op jit(solution)/shard_map/pallas_call | solution.py:371
  75.2 2.4 %shard_map.29 = f32[64,4,8,128]{3,2,1,0:T(8,128)} custom-call(f32[256,256]{1,0:T(8,128)S(1)} %get-tuple-element.7.w, f32[4,4,8,8,8,128]{5,4,3,2,1,0:T(8,128)S(1)} %get-tuple-element.8.gall), custom_call_target="tpu_custom_call" | custom-call | tf_op jit(solution)/shard_map/pallas_call | solution.py:406

commit v6 on v5

--- a/solution.py
+++ b/solution.py
@@ -17,7 +17,7 @@
 NCELLS = 256 * 8 * 128
 GROUP = 4
 
-SPLIT = (0, 1, 1, 4)
+SPLIT = (0, 2, 2, 4)
 
 
 def nt(a, b):
@@ -60,9 +60,9 @@
 
 def main_kernel(orb_hbm, pot_hbm, w, gall, x_in, stage, vbuf, ybuf, abuf, fbuf, zmat, pots,
                 mt, pair_in, half_sum, layer_in, zsum, mg,
-                in_sem, pot_in, pot_send, pot_recv, x_send, x_recv, first_send, first_recv, first_out, h_send, h_recv, a_send, a_recv,
+                in_sem, pot_in, pot_send, pot_recv, x_send, x_recv, first_recv, h_send, h_recv, a_send, a_recv,
                 pair_send, pair_recv, layer_send, layer_recv, z_send, z_recv,
-                spread_send, spread_recv, back_send, back_recv, ga_send, ga_recv):
+                spread_send, spread_recv, back_send, back_recv, ga_send, ga_recv, far_recv):
     b = lax.axis_index("band")
     g = lax.axis_index("grid")
     hi = lax.rem(g, 2)
@@ -117,7 +117,6 @@
 
     far = lax.rem(b + 2, 4)
     sib = b + 1 - 2 * core
-    x_copies = []
 
     def turn(c):
         for h in range(2):
@@ -129,37 +128,27 @@
         for h in range(2):
             if c == 0:
                 for t in range(4):
-                    item = copy(stage.at[h, 0, t], vbuf.at[0, 8 + 4 * hi + t], first_send.at[h, t], first_recv.at[t], dev(far, m * 2 + h))
+                    item = copy(stage.at[h, 0, t], vbuf.at[0, 8 + 4 * hi + t], x_send, first_recv.at[t], dev(far, m * 2 + h))
                     item.start()
-                    x_copies.append(item)
                 continue
-            item = copy(stage.at[h, c], vbuf.at[c, pl.ds(8 + 4 * hi, 4)], x_send.at[h, c], x_recv.at[c], dev(far, m * 2 + h))
+            item = copy(stage.at[h, c], vbuf.at[c, pl.ds(8 + 4 * hi, 4)], x_send, x_recv.at[c], dev(far, m * 2 + h))
             item.start()
-            x_copies.append(item)
-
-    h_copies = {}
 
     def send_halo(c):
         if c == 0:
-            h_copies[0] = []
             for t in range(4):
                 await_bytes(vbuf.at[0, pl.ds(8, 2)], first_recv.at[t])
                 for side in range(2):
                     for k in range(2):
                         at = 16 * side + 4 * k + t
-                        item = copy(vbuf.at[0, 8 + 4 * k + t], vbuf.at[0, at], first_out.at[t, k, side],
+                        item = copy(vbuf.at[0, 8 + 4 * k + t], vbuf.at[0, at], h_send.at[0],
                                     h_recv.at[0, side], dev(b, (down if side else up) * 2 + hi))
                         item.start()
-                        h_copies[0].append(item)
             return
         await_bytes(vbuf.at[c, pl.ds(8, 8)], x_recv.at[c])
         own = vbuf.at[c, pl.ds(8, 8)]
-        h_copies[c] = [
-            copy(own, vbuf.at[c, pl.ds(0, 8)], h_send.at[c, 0], h_recv.at[c, 0], dev(b, up * 2 + hi)),
-            copy(own, vbuf.at[c, pl.ds(16, 8)], h_send.at[c, 1], h_recv.at[c, 1], dev(b, down * 2 + hi)),
-        ]
-        for item in h_copies[c]:
-            item.start()
+        copy(own, vbuf.at[c, pl.ds(0, 8)], h_send.at[c], h_recv.at[c, 0], dev(b, up * 2 + hi)).start()
+        copy(own, vbuf.at[c, pl.ds(16, 8)], h_send.at[c], h_recv.at[c, 1], dev(b, down * 2 + hi)).start()
 
     turn(0)
     zmat[...] = circulant()
@@ -169,9 +158,9 @@
     pot_load.wait()
     side = lax.rem(m + 2 * hi + 31, 32)
     pot_copies = [
-        copy(pots.at[1 + hi], pots.at[1 + hi], pot_send.at[0], pot_recv, dev(b, m * 2 + 1 - hi)),
-        copy(pots.at[1 + hi], pots.at[3 - 3 * hi], pot_send.at[1], pot_recv, dev(b, side * 2)),
-        copy(pots.at[1 + hi], pots.at[3 - 3 * hi], pot_send.at[2], pot_recv, dev(b, side * 2 + 1)),
+        copy(pots.at[1 + hi], pots.at[1 + hi], pot_send, pot_recv, dev(b, m * 2 + 1 - hi)),
+        copy(pots.at[1 + hi], pots.at[3 - 3 * hi], pot_send, pot_recv, dev(b, side * 2)),
+        copy(pots.at[1 + hi], pots.at[3 - 3 * hi], pot_send, pot_recv, dev(b, side * 2 + 1)),
     ]
     for item in pot_copies:
         item.start()
@@ -196,8 +185,8 @@
     def gather(lo, hi_):
         for k in range(lo, hi_):
             own = piece(b, k)
-            to_far.append(copy(own, own, ga_send.at[1, k], ga_recv.at[1, k], dev(far, g)))
-            to_sib.append(copy(own, own, ga_send.at[0, k], ga_recv.at[0, k], dev(sib, g)))
+            to_far.append(copy(own, own, ga_send.at[1], far_recv.at[k], dev(far, g)))
+            to_sib.append(copy(own, own, ga_send.at[0], ga_recv.at[0], dev(sib, g)))
             to_far[k].start()
             to_sib[k].start()
 
@@ -205,10 +194,9 @@
         for k in range(lo, hi_):
             to_far[k].wait_recv()
             theirs = piece(far, k)
-            relay.append(copy(theirs, theirs, ga_send.at[2, k], ga_recv.at[2, k], dev(sib, g)))
+            relay.append(copy(theirs, theirs, ga_send.at[2], ga_recv.at[1], dev(sib, g)))
             relay[k].start()
 
-    a_copies = []
     row = far * 2 + hi
     for c in range(4):
         await_bytes(vbuf.at[c, pl.ds(0, 8)], h_recv.at[c, 0])
@@ -229,9 +217,8 @@
             fbuf[c, pl.ds(t, 4)] = 2.0 * step - vbuf[c, pl.ds(t + 8, 4)]
             for i in range(n, 4):
                 bb = lax.rem(b + i, 4)
-                item = copy(fbuf.at[c, t + bb], gall.at[bb, c, row], a_send.at[c, 4 * n + i], a_recv.at[c], dev(bb, m * 2 + half))
+                item = copy(fbuf.at[c, t + bb], gall.at[bb, c, row], a_send.at[c], a_recv.at[c], dev(bb, m * 2 + half))
                 item.start()
-                a_copies.append(item)
         pltpu.make_async_copy(fbuf.at[c, p], gall.at[b, c, row], a_recv.at[c]).start()
         if c >= 1:
             await_bytes(gall.at[b, c - 1], a_recv.at[c - 1])
@@ -239,7 +226,6 @@
             gather(SPLIT[c - 1], SPLIT[c])
     await_bytes(gall.at[b, 3], a_recv.at[3])
 
-    sends = []
     acc = None
     for pair in range(4):
         a = orbitals_of(gall, b, pair)
@@ -250,15 +236,13 @@
         mt[half] = acc[:, half * 128:half * 128 + 128].reshape(16, 2, 8, 128)
     item = copy(mt.at[1 - core], pair_in, pair_send, pair_recv, dev(sib, g))
     item.start()
-    sends.append(item)
-
-    sends[0].wait_recv()
+
+    item.wait_recv()
     half_sum[...] = mt[core] + pair_in[...]
     for i in range(1, 16):
         q, target = layer(i)
-        item = copy(half_sum.at[q], layer_in.at[i - 1], layer_send.at[i - 1], layer_recv, target)
+        item = copy(half_sum.at[q], layer_in.at[i - 1], layer_send, layer_recv, target)
         item.start()
-        sends.append(item)
     gather(SPLIT[2], SPLIT[3])
     await_bytes(layer_in, layer_recv)
     total = half_sum[chip]
@@ -267,9 +251,8 @@
     zsum[z] = total
     for i in range(1, 8):
         q, target = zring(i)
-        item = copy(zsum.at[z], zsum.at[z], z_send.at[i - 1], z_recv, target)
+        item = copy(zsum.at[z], zsum.at[z], z_send, z_recv, target)
         item.start()
-        sends.append(item)
     await_bytes(zsum.at[pl.ds(0, 7)], z_recv)
     total = zsum[0]
     for i in range(1, 8):
@@ -277,14 +260,20 @@
     mg[core, chip] = total
     for i in range(1, 16):
         q, target = layer(i)
-        item = copy(mg.at[core, chip], mg.at[core, chip], spread_send.at[i - 1], spread_recv, target)
+        item = copy(mg.at[core, chip], mg.at[core, chip], spread_send, spread_recv, target)
         item.start()
-        sends.append(item)
     gather(SPLIT[3], 8)
+    await_bytes(pots.at[pl.ds(0, 3)], pot_send)
+    await_bytes(stage, x_send)
+    for c in range(4):
+        await_bytes(vbuf.at[c, pl.ds(0, 16)], h_send.at[c])
+        await_bytes(fbuf.at[c, pl.ds(0, 7)], a_send.at[c])
+    await_bytes(mt.at[0], pair_send)
+    await_bytes(layer_in, layer_send)
+    await_bytes(zsum.at[pl.ds(0, 7)], z_send)
     await_bytes(layer_in, spread_recv)
     item = copy(mg.at[core], mg.at[core], back_send, back_recv, dev(sib, g))
     item.start()
-    sends.append(item)
     item.wait_recv()
 
     pass_on(0, SPLIT[3])
@@ -298,14 +287,12 @@
     w[128:256, 128:256] = w22
     pass_on(6, 8)
 
-    for k in range(8):
-        to_sib[k].wait_recv()
-        relay[k].wait_recv()
-    for item in pot_copies + x_copies + a_copies + sends + to_sib + to_far + relay:
-        item.wait_send()
-    for c in range(4):
-        for item in h_copies[c]:
-            item.wait_send()
+    await_bytes(layer_in, spread_send)
+    await_bytes(mt.at[0], back_send)
+    await_bytes(gall.at[sib], ga_recv.at[0])
+    await_bytes(gall.at[lax.rem(sib + 2, 4)], ga_recv.at[1])
+    for k in range(3):
+        await_bytes(gall.at[b], ga_send.at[k])
 
 
 def inverse_factor(block):
@@ -345,13 +332,22 @@
     return jnp.concatenate([jnp.where(lane <= sub + 8 * i, groups[i], 0.0) for i in range(16)], axis=0)
 
 
+def split(a):
+    top = a.astype(jnp.bfloat16)
+    return top, (a - top.astype(jnp.float32)).astype(jnp.bfloat16)
+
+
 def product_kernel(w, gall, out_hbm, res, out_sem):
     b = lax.axis_index("band")
-    mine = w[pl.ds(pl.multiple_of(b * 64, 64), 64), :]
+    mine = jnp.concatenate(split(w[pl.ds(pl.multiple_of(b * 64, 64), 64), :]), axis=0)
     outs = []
     for t in range(4):
         for pair in range(4):
-            block = lax.dot_general(mine, orbitals_of(gall, t, pair), (((1,), (0,)), ((), ())), precision=lax.Precision.HIGH, preferred_element_type=jnp.float32)
+            top, low = split(orbitals_of(gall, t, pair))
+            dims = (((1,), (0,)), ((), ()))
+            both = (lax.dot_general(mine, top, dims, preferred_element_type=jnp.float32)
+                    + lax.dot_general(mine, low, dims, preferred_element_type=jnp.float32))
+            block = both[:64] + both[64:]
             res[t, :, 2 * pair, :] = block[:, :128]
             res[t, :, 2 * pair + 1, :] = block[:, 128:]
         item = pltpu.make_async_copy(res.at[t], out_hbm.at[:, t], out_sem.at[t])
@@ -389,17 +385,17 @@
             pltpu.VMEM((8, 2, 8, 128), f32),
             pltpu.VMEM((2, 16, 2, 8, 128), f32),
             dma((2, 4)), dma,
-            dma((3,)), dma,
-            dma((2, 4)), dma((4,)),
-            dma((2, 4)), dma((4,)), dma((4, 2, 2)),
-            dma((4, 2)), dma((4, 2)),
-            dma((4, 8)), dma((4,)),
-            dma, dma,
-            dma((15,)), dma,
-            dma((7,)), dma,
-            dma((15,)), dma,
-            dma, dma,
-            dma((3, 8)), dma((3, 8)),
+            dma, dma,
+            dma, dma((4,)),
+            dma((4,)),
+            dma((4,)), dma((4, 2)),
+            dma((4,)), dma((4,)),
+            dma, dma,
+            dma, dma,
+            dma, dma,
+            dma, dma,
+            dma, dma,
+            dma((3,)), dma((2,)), dma((8,)),
         ],
         compiler_params=pltpu.CompilerParams(collective_id=0, has_side_effects=True, vmem_limit_bytes=40 * 2**20),
     )(orbitals, potential)

time: 77.9 us -> 76.3 us (0.979)
  Pallas kernels: 77.6 us -> 76 us
    pallas_call x1, Pallas kernels: 75.2 us -> 74 us  [body(): pl.pallas_call(main_kernel, out_shape=(jax.ShapeDtypeStruct((256, 256), f...]
where the time goes in v6:
time: 76.3 us; the launch traced here: 76.2 us
  Pallas kernels  76 us (100%)
    pallas_call x1, Pallas kernels, body(): pl.pallas_call(main_kernel, out_shape=(jax.ShapeDtypeStruct((256, 256), f...  74 us
    pallas_call x1, Pallas kernels, body(): pl.pallas_call(product_kernel, out_shape=jax.ShapeDtypeStruct(orbitals.sh...  1.96 us

profile of v6, /device:TPU:1, one launch (start us, length us, event | category | flops | bytes accessed | tf_op | source)
XLA Modules:
  0.0 76.2 jit_solution(9634744242707649476)
XLA Ops:
  0.0 74.0 %shard_map.28 = (f32[256,256]{1,0:T(8,128)S(1)}, f32[4,4,8,8,8,128]{5,4,3,2,1,0:T(8,128)S(1)}) custom-call(f32[64,4,8,128]{3,2,1,0:T(8,128)} %orb_hbm.1, f32[4,8,128]{2,1,0:T(8,128)} %pot_hbm.1), custom_call_target="tpu_custom_call" | custom-call | tf_op jit(solution)/shard_map/pallas_call | solution.py:367
  74.0 2.0 %shard_map.29 = f32[64,4,8,128]{3,2,1,0:T(8,128)} custom-call(f32[256,256]{1,0:T(8,128)S(1)} %get-tuple-element.7.w, f32[4,4,8,8,8,128]{5,4,3,2,1,0:T(8,128)S(1)} %get-tuple-element.8.gall), custom_call_target="tpu_custom_call" | custom-call | tf_op jit(solution)/shard_map/pallas_call | solution.py:402

commit v7 on v6

--- a/solution.py
+++ b/solution.py
@@ -35,7 +35,7 @@
 def circulant():
     i = lax.broadcasted_iota(jnp.int32, (128, 128), 0)
     j = lax.broadcasted_iota(jnp.int32, (128, 128), 1)
-    apart = lax.rem(i - j + 128, 128)
+    apart = (i - j) & 127
     total = jnp.zeros((128, 128), jnp.float32)
     for k in range(1, 5):
         total = jnp.where((apart == k) | (apart == 128 - k), TAPS[k], total)
@@ -59,7 +59,7 @@
 
 
 def main_kernel(orb_hbm, pot_hbm, w, gall, x_in, stage, vbuf, ybuf, abuf, fbuf, zmat, pots,
-                mt, pair_in, half_sum, layer_in, zsum, mg,
+                mt, pair_in, half_sum, layer_in, zsum, mg, columns,
                 in_sem, pot_in, pot_send, pot_recv, x_send, x_recv, first_recv, h_send, h_recv, a_send, a_recv,
                 pair_send, pair_recv, layer_send, layer_recv, z_send, z_recv,
                 spread_send, spread_recv, back_send, back_recv, ga_send, ga_recv, far_recv):
@@ -97,6 +97,16 @@
         zz = lax.rem(z + i, 8)
         return zz, dev(b, zz * 8 + y * 2 + hi)
 
+    loads = []
+
+    def load(lo, hi_):
+        for c in range(lo, hi_):
+            for h in range(2):
+                item = pltpu.make_async_copy(orb_hbm.at[pl.ds(h * 32 + c * 8, 8)], x_in.at[h, c], in_sem.at[h, c])
+                item.start()
+                loads.append(item)
+
+    load(0, 1)
     other = lax.rem(g + 63 + 2 * hi, 64)
     barrier = pltpu.get_barrier_semaphore()
     peers = [zring(i)[1] for i in (4, 3, 5, 2, 6, 1, 7)]
@@ -106,14 +116,9 @@
     for peer in peers:
         pl.semaphore_signal(barrier, inc=1, device_id=peer, device_id_type=MESH)
 
+    load(1, 4)
     pot_load = pltpu.make_async_copy(pot_hbm, pots.at[1 + hi], pot_in)
     pot_load.start()
-    loads = []
-    for c in range(4):
-        for h in range(2):
-            load = pltpu.make_async_copy(orb_hbm.at[pl.ds(h * 32 + c * 8, 8)], x_in.at[h, c], in_sem.at[h, c])
-            load.start()
-            loads.append(load)
 
     far = lax.rem(b + 2, 4)
     sib = b + 1 - 2 * core
@@ -151,7 +156,6 @@
         copy(own, vbuf.at[c, pl.ds(16, 8)], h_send.at[c], h_recv.at[c, 1], dev(b, down * 2 + hi)).start()
 
     turn(0)
-    zmat[...] = circulant()
     pl.semaphore_wait(barrier, len(peers))
     send_x(0)
 
@@ -170,6 +174,7 @@
     turn(3)
     send_halo(0)
     send_x(2)
+    zmat[...] = circulant()
     await_bytes(pots.at[pl.ds(0, 3)], pot_recv)
     for t in range(16):
         a = pots[t // 4, t % 4] * (1.0 / HALF) + (3.0 * TAPS[0] - CENTER / HALF)
@@ -277,10 +282,10 @@
     item.wait_recv()
 
     pass_on(0, SPLIT[3])
-    w11 = inverse_factor(mg[0, 0:8].reshape(128, 128))
+    w11 = inverse_factor(mg[0, 0:8].reshape(128, 128), columns)
     pass_on(SPLIT[3], 6)
     l21 = nt(mg[0, 8:16].reshape(128, 128), w11)
-    w22 = inverse_factor(mg[1, 8:16].reshape(128, 128) - nt(l21, l21))
+    w22 = inverse_factor(mg[1, 8:16].reshape(128, 128) - nt(l21, l21), columns)
     w[0:128, 0:128] = w11
     w[0:128, 128:256] = jnp.zeros((128, 128), jnp.float32)
     w[128:256, 0:128] = -nn(w22, nn(l21, w11))
@@ -295,7 +300,7 @@
         await_bytes(gall.at[b], ga_send.at[k])
 
 
-def inverse_factor(block):
+def inverse_factor(block, columns):
     lane = lax.broadcasted_iota(jnp.int32, (8, 128), 1)
     sub = lax.broadcasted_iota(jnp.int32, (8, 128), 0)
     groups = [block[8 * i:8 * i + 8] for i in range(16)]
@@ -305,8 +310,9 @@
         d = [[None] * 8 for _ in range(8)]
         for j in range(8):
             column = jnp.broadcast_to(panel[:, base + j:base + j + 1], (8, 128))
+            columns[n % 2, j] = column
             for i in range(j, 8):
-                d[i][j] = jnp.broadcast_to(column[i:i + 1], (8, 128))
+                d[i][j] = columns[n % 2, j, pl.ds(i, 8, stride=0), :]
         inside = (lane >= base) & (lane < base + 8)
         masked = jnp.where(inside, jnp.where(lane == base + sub, 1.0, 0.0), panel)
         rows = [jnp.broadcast_to(masked[k:k + 1], (8, 128)) for k in range(8)]
@@ -384,6 +390,7 @@
             pltpu.VMEM((15, 2, 8, 128), f32),
             pltpu.VMEM((8, 2, 8, 128), f32),
             pltpu.VMEM((2, 16, 2, 8, 128), f32),
+            pltpu.VMEM((2, 8, 8, 128), f32),
             dma((2, 4)), dma,
             dma, dma,
             dma, dma((4,)),

time: 76.3 us -> 75.2 us (0.986)
  Pallas kernels: 76 us -> 75.1 us
    pallas_call x1, Pallas kernels: 74 us -> 73.1 us  [body(): pl.pallas_call(main_kernel, out_shape=(jax.ShapeDtypeStruct((256, 256), f...]
where the time goes in v7:
time: 75.2 us; the launch traced here: 75.1 us
  Pallas kernels  75.1 us (100%)
    pallas_call x1, Pallas kernels, body(): pl.pallas_call(main_kernel, out_shape=(jax.ShapeDtypeStruct((256, 256), f...  73.1 us
    pallas_call x1, Pallas kernels, body(): pl.pallas_call(product_kernel, out_shape=jax.ShapeDtypeStruct(orbitals.sh...  1.96 us

profile of v7, /device:TPU:1, one launch (start us, length us, event | category | flops | bytes accessed | tf_op | source)
XLA Modules:
  0.0 75.1 jit_solution(2127246692725706202)
XLA Ops:
  0.0 73.1 %shard_map.28 = (f32[256,256]{1,0:T(8,128)S(1)}, f32[4,4,8,8,8,128]{5,4,3,2,1,0:T(8,128)S(1)}) custom-call(f32[64,4,8,128]{3,2,1,0:T(8,128)} %orb_hbm.1, f32[4,8,128]{2,1,0:T(8,128)} %pot_hbm.1), custom_call_target="tpu_custom_call" | custom-call | tf_op jit(solution)/shard_map/pallas_call | solution.py:373
  73.1 2.0 %shard_map.29 = f32[64,4,8,128]{3,2,1,0:T(8,128)} custom-call(f32[256,256]{1,0:T(8,128)S(1)} %get-tuple-element.7.w, f32[4,4,8,8,8,128]{5,4,3,2,1,0:T(8,128)S(1)} %get-tuple-element.8.gall), custom_call_target="tpu_custom_call" | custom-call | tf_op jit(solution)/shard_map/pallas_call | solution.py:409

commit v8 on v7

--- a/solution.py
+++ b/solution.py
@@ -310,7 +310,7 @@
         d = [[None] * 8 for _ in range(8)]
         for j in range(8):
             column = jnp.broadcast_to(panel[:, base + j:base + j + 1], (8, 128))
-            columns[n % 2, j] = column
+            columns[n % 2, j, 0:8] = column
             for i in range(j, 8):
                 d[i][j] = columns[n % 2, j, pl.ds(i, 8, stride=0), :]
         inside = (lane >= base) & (lane < base + 8)
@@ -390,7 +390,7 @@
             pltpu.VMEM((15, 2, 8, 128), f32),
             pltpu.VMEM((8, 2, 8, 128), f32),
             pltpu.VMEM((2, 16, 2, 8, 128), f32),
-            pltpu.VMEM((2, 8, 8, 128), f32),
+            pltpu.VMEM((2, 8, 16, 128), f32),
             dma((2, 4)), dma,
             dma, dma,
             dma, dma((4,)),

time: 75.2 us -> 75.2 us (level)
  no operation moved by 1% of the time
where the time goes in v8:
time: 75.2 us; the launch traced here: 75.1 us
  Pallas kernels  75.1 us (100%)
    pallas_call x1, Pallas kernels, body(): pl.pallas_call(main_kernel, out_shape=(jax.ShapeDtypeStruct((256, 256), f...  73.1 us
    pallas_call x1, Pallas kernels, body(): pl.pallas_call(product_kernel, out_shape=jax.ShapeDtypeStruct(orbitals.sh...  1.96 us

profile of v8, /device:TPU:1, one launch (start us, length us, event | category | flops | bytes accessed | tf_op | source)
XLA Modules:
  0.0 75.1 jit_solution(18409504636560453863)
XLA Ops:
  0.0 73.1 %shard_map.28 = (f32[256,256]{1,0:T(8,128)S(1)}, f32[4,4,8,8,8,128]{5,4,3,2,1,0:T(8,128)S(1)}) custom-call(f32[64,4,8,128]{3,2,1,0:T(8,128)} %orb_hbm.1, f32[4,8,128]{2,1,0:T(8,128)} %pot_hbm.1), custom_call_target="tpu_custom_call" | custom-call | tf_op jit(solution)/shard_map/pallas_call | solution.py:373
  73.1 2.0 %shard_map.29 = f32[64,4,8,128]{3,2,1,0:T(8,128)} custom-call(f32[256,256]{1,0:T(8,128)S(1)} %get-tuple-element.7.w, f32[4,4,8,8,8,128]{5,4,3,2,1,0:T(8,128)S(1)} %get-tuple-element.8.gall), custom_call_target="tpu_custom_call" | custom-call | tf_op jit(solution)/shard_map/pallas_call | solution.py:409

commit v9 on v8

--- a/solution.py
+++ b/solution.py
@@ -285,10 +285,11 @@
     w11 = inverse_factor(mg[0, 0:8].reshape(128, 128), columns)
     pass_on(SPLIT[3], 6)
     l21 = nt(mg[0, 8:16].reshape(128, 128), w11)
+    cross = nn(l21, w11)
     w22 = inverse_factor(mg[1, 8:16].reshape(128, 128) - nt(l21, l21), columns)
     w[0:128, 0:128] = w11
     w[0:128, 128:256] = jnp.zeros((128, 128), jnp.float32)
-    w[128:256, 0:128] = -nn(w22, nn(l21, w11))
+    w[128:256, 0:128] = -nn(w22, cross)
     w[128:256, 128:256] = w22
     pass_on(6, 8)
 

time: 75.2 us -> 75.3 us (level)
  no operation moved by 1% of the time
where the time goes in v9:
time: 75.3 us; the launch traced here: 75.2 us
  Pallas kernels  75.2 us (100%)
    pallas_call x1, Pallas kernels, body(): pl.pallas_call(main_kernel, out_shape=(jax.ShapeDtypeStruct((256, 256), f...  73.2 us
    pallas_call x1, Pallas kernels, body(): pl.pallas_call(product_kernel, out_shape=jax.ShapeDtypeStruct(orbitals.sh...  1.96 us

profile of v9, /device:TPU:1, one launch (start us, length us, event | category | flops | bytes accessed | tf_op | source)
XLA Modules:
  0.0 75.2 jit_solution(3797209553114917208)
XLA Ops:
  0.0 73.2 %shard_map.28 = (f32[256,256]{1,0:T(8,128)S(1)}, f32[4,4,8,8,8,128]{5,4,3,2,1,0:T(8,128)S(1)}) custom-call(f32[64,4,8,128]{3,2,1,0:T(8,128)} %orb_hbm.1, f32[4,8,128]{2,1,0:T(8,128)} %pot_hbm.1), custom_call_target="tpu_custom_call" | custom-call | tf_op jit(solution)/shard_map/pallas_call | solution.py:374
  73.2 2.0 %shard_map.29 = f32[64,4,8,128]{3,2,1,0:T(8,128)} custom-call(f32[256,256]{1,0:T(8,128)S(1)} %get-tuple-element.7.w, f32[4,4,8,8,8,128]{5,4,3,2,1,0:T(8,128)S(1)} %get-tuple-element.8.gall), custom_call_target="tpu_custom_call" | custom-call | tf_op jit(solution)/shard_map/pallas_call | solution.py:410
